TPU v7x, 128 devices: a whole 4x4x4 slice. The times are simulated.
128 devices in a mesh: seq: 16 (over z, x_hi, core), head: 8 (over y, x_lo).
Axes of the slice: x: 4 (x_hi: 2, x_lo: 2; x = x_hi * 2 + x_lo), y: 4, z: 4, core: 2. Of those that a mesh axis runs over, the one named last changes fastest.
Arguments:
- x_values: bfloat16 [16384, 16384], P('seq', 'head'), may hold values from -6 to 6
- bc_values: bfloat16 [2, 16384, 2048], P(None, 'seq', 'head'), may hold values from -6 to 6
- z_values: bfloat16 [16384, 16384], P('seq', 'head'), may hold values from -12 to 12
- dt_values: bfloat16 [16384, 256], P('seq', 'head'), may hold values from -4 to 4
- xconv_weight: float32 [4, 16384], P(None, 'head'), may hold values from -3 to 3
- bconv_weight: float32 [2, 4, 2048], P(None, None, 'head'), may hold values from -3 to 3
- xconv_bias: float32 [16384], P('head'), may hold values from -0.5 to 0.5
- bconv_bias: float32 [2, 2048], P(None, 'head'), may hold values from -0.5 to 0.5
- dt_offset: float32 [256], P('head'), may hold values from -16 to -3
- decay_log: float32 [256], P('head'), may hold values from 0 to 3
- skip_gain: float32 [256], P('head'), may hold values from 0.5 to 2
- norm_gain: float32 [16384], P('head'), may hold values from 0.1 to 1.9
- out_weight: bfloat16 [16384, 4096], P('head'), may hold values from -0.046875 to 0.046875
Outputs:
- mixer_out: bfloat16 [16384, 4096], P(('seq', 'head'))
All inputs are finite; a program needn't handle non-finite values.
Results may differ from a plain program's by a relative error of at most 0.015.
Values may be sent and summed in bfloat16 or wider, within the bound.
A program may use at most 256 MiB of HBM per device.

v0:
```python
import jax
import jax.numpy as jnp
from jax import lax
from jax.sharding import PartitionSpec as P

H = 256
P_SIZE = 64
N = 256
G = 8
KW = 4
BLOCK = 128


def shifted(value, axis, by):
    devices = lax.axis_size(axis)
    pairs = [(i, i + by) for i in range(devices) if 0 <= i + by < devices]
    return lax.ppermute(value, axis, pairs)


def conv_silu(extended, weight, bias, length):
    padded = extended.astype(jnp.float32)
    total = jnp.zeros((length, extended.shape[1]), jnp.float32) + bias[None, :]
    for offset in range(KW):
        total = total + weight[offset][None, :] * padded[offset : offset + length]
    return jax.nn.silu(total).astype(jnp.bfloat16)


def per_device(
    x_values,
    bc_values,
    z_values,
    dt_values,
    xconv_weight,
    bconv_weight,
    xconv_bias,
    bconv_bias,
    dt_offset,
    decay_log,
    skip_gain,
    norm_gain,
    out_weight,
):
    rows_here = x_values.shape[0]
    heads_here = dt_values.shape[1]
    groups_here = bc_values.shape[2] // N
    per_group = H // G
    blocks = rows_here // BLOCK
    margin = KW - 1
    prev_x, prev_bc = shifted(
        (x_values[rows_here - margin :], bc_values[:, rows_here - margin :]), "seq", 1
    )
    x_conv = conv_silu(
        jnp.concatenate([prev_x, x_values], axis=0), xconv_weight, xconv_bias, rows_here
    )
    b_conv = conv_silu(
        jnp.concatenate([prev_bc[0], bc_values[0]], axis=0),
        bconv_weight[0],
        bconv_bias[0],
        rows_here,
    )
    c_conv = conv_silu(
        jnp.concatenate([prev_bc[1], bc_values[1]], axis=0),
        bconv_weight[1],
        bconv_bias[1],
        rows_here,
    )
    steps_dt = jax.nn.softplus(dt_values.astype(jnp.float32) + dt_offset[None, :])
    log_decay = steps_dt * (-jnp.exp(decay_log))[None, :]
    x_blocks = x_conv.reshape(blocks, BLOCK, groups_here, per_group, P_SIZE)
    b_blocks = b_conv.reshape(blocks, BLOCK, groups_here, N)
    c_blocks = c_conv.reshape(blocks, BLOCK, groups_here, N)
    dt_blocks = jnp.transpose(steps_dt.reshape(blocks, BLOCK, groups_here, per_group), (0, 2, 3, 1))
    cumul = jnp.cumsum(
        jnp.transpose(log_decay.reshape(blocks, BLOCK, groups_here, per_group), (0, 2, 3, 1)),
        axis=3,
    )
    positions = jnp.arange(BLOCK)
    causal = positions[:, None] >= positions[None, :]
    inner = jnp.einsum("ctgn,csgn->cgts", c_blocks, b_blocks, preferred_element_type=jnp.float32)
    diff = cumul[..., :, None] - cumul[..., None, :]
    weights = jnp.where(causal, jnp.exp(jnp.where(causal, diff, 0.0)), 0.0)
    scores = (inner[:, :, None] * weights * dt_blocks[..., None, :]).astype(jnp.bfloat16)
    y_intra = jnp.einsum("cghts,csghp->ctghp", scores, x_blocks, preferred_element_type=jnp.float32)
    to_end = jnp.exp(cumul[..., -1:] - cumul) * dt_blocks
    x_weighted = (
        x_blocks.astype(jnp.float32) * jnp.transpose(to_end, (0, 3, 1, 2))[..., None]
    ).astype(jnp.bfloat16)
    states = jnp.einsum(
        "csghp,csgn->cghpn", x_weighted, b_blocks, preferred_element_type=jnp.float32
    )
    block_total = cumul[..., -1]
    block_decay = jnp.exp(block_total)

    def advance(carry, item):
        decay, state = item
        return (decay[..., None, None] * carry + state, carry)

    local_end, local_before = lax.scan(
        advance, jnp.zeros((groups_here, per_group, P_SIZE, N), jnp.float32), (block_decay, states)
    )
    device_decay = jnp.prod(block_decay, axis=0)

    def pass_on(index, arriving):
        leaving = device_decay[..., None, None] * arriving + local_end
        return shifted(leaving.astype(jnp.bfloat16), "seq", 1).astype(leaving.dtype)

    incoming = lax.fori_loop(0, lax.axis_size("seq") - 1, pass_on, jnp.zeros_like(local_end))
    lead = jnp.cumsum(block_total, axis=0) - block_total
    before = (local_before + jnp.exp(lead)[..., None, None] * incoming[None]).astype(jnp.bfloat16)
    y_state = jnp.transpose(jnp.exp(cumul), (0, 3, 1, 2))[..., None] * jnp.einsum(
        "ctgn,cghpn->ctghp", c_blocks, before, preferred_element_type=jnp.float32
    )
    skip_here = skip_gain.reshape(groups_here, per_group)
    total = y_intra + y_state + skip_here[None, None, :, :, None] * x_blocks.astype(jnp.float32)
    width = per_group * P_SIZE
    gated = total.reshape(rows_here, groups_here, width) * jax.nn.silu(
        z_values.astype(jnp.float32).reshape(rows_here, groups_here, width)
    )
    scale = lax.rsqrt(jnp.mean(gated * gated, axis=2, keepdims=True) + 1e-05)
    normed = (
        (gated * scale * norm_gain.reshape(groups_here, width)[None])
        .astype(jnp.bfloat16)
        .reshape(rows_here, heads_here * P_SIZE)
    )
    summed = lax.psum_scatter(
        jnp.dot(normed, out_weight, preferred_element_type=jnp.float32).astype(jnp.bfloat16),
        "head",
        scatter_dimension=0,
        tiled=True,
    )
    return summed


def solution(mesh):
    return jax.shard_map(
        per_device,
        mesh=mesh,
        in_specs=(
            P("seq", "head"),
            P(None, "seq", "head"),
            P("seq", "head"),
            P("seq", "head"),
            P(None, "head"),
            P(None, None, "head"),
            P("head"),
            P(None, "head"),
            P("head"),
            P("head"),
            P("head"),
            P("head"),
            P("head", None),
        ),
        out_specs=P(("seq", "head"), None),
        check_vma=False,
    )
```

profile of v0, /device:TPU:1, one launch (start us, length us, event | category | flops | bytes accessed | tf_op | source)
XLA Modules:
  0.0 721.5 jit_solution(7203944131117533871)
XLA Ops:
  7.8 6.0 collective-permute-start.2
  30.1 6.4 copy.20
  37.3 6.4 copy.30
  50.8 10.2 %convert_bitcast_fusion = (f32[256,8,8,128]{3,1,2,0:T(8,128)}, bf16[1024,2048]{0,1:T(8,128)(2,1)S(1)}) fusion(f32[1027,2048]{0,1:T(8,128)S(1)} %maximum_convert_fusion, f32[2048]{0:T(1024)S(1)} %bitcast.149, f32[2048]{0:T(1024)S(1)} %bitcast.150, f32[2048]{0:T(1024)S(1)} %bitcast.148, f32[2048]{0:T(1024)S(1)} %bitcast.147, f32[2048]{0:T(1024)S(1)} %copy-done.13), kind=kLoop, calls=%fused_computation.31 | loop fusion | flops 29360128 | bytes 46178304
  65.4 8.1 %convolution_bitcast_fusion = f32[8,1,32,64,256]{4,3,2,1,0:T(8,128)} fusion(bf16[8,128,256,1]{2,1,3,0:T(8,128)(2,1)S(1)} %bitcast.140, bf16[8,128,32,64]{1,0,3,2:T(8,128)(2,1)S(1)} %multiply_convert_fusion.3), kind=kOutput, calls=%fused_computation.11 | convolution fusion | flops 1073741824 | bytes 21495808 | tf_op jit(solution)/shard_map/csghp,csgn->cghpn/dot_general | solution.py:88
  73.5 44.6 %while.24 = (s32[]{:T(128)}, f32[1,32,64,256]{3,2,1,0:T(8,128)S(1)}, f32[8,1,32,64,256]{4,3,2,1,0:T(8,128)}, f32[8,1,32]{2,1,0:T(1,128)}, f32[8,1,32,64,256]{4,3,2,1,0:T(8,128)}, /*index=5*/s32[]{:T(128)}, s32[]{:T(128)}) while((s32[]{:T(128)}, f32[1,32,64,256]{3,2,1,0:T(8,128)S(1)}, f32[8,1,32,64,256]{4,3,2,1,0:T(8,128)}, ...), condition=%wide.region_2.3_spmd.clone, body=%wide.region_1.2_spmd.clone.sunk | while | flops 2097155 | bytes 10486752 | solution.py:98
  118.1 8.7 %copy.36 = f32[256,8,8,128]{3,2,1,0:T(8,128)} copy(f32[256,8,8,128]{3,1,2,0:T(8,128)} %get-tuple-element.122) | data formatting | bytes 16777216
  126.8 329.7 %while.25 = (s32[]{:T(128)}, f32[1,32,64,256]{3,2,1,0:T(8,128)}, f32[1,32]{1,0:T(1,128)S(1)}, f32[1,32,64,256]{3,2,1,0:T(8,128)S(1)}, s32[]{:T(128)}, /*index=5*/s32[]{:T(128)}) while((s32[]{:T(128)}, f32[1,32,64,256]{3,2,1,0:T(8,128)}, f32[1,32]{1,0:T(1,128)S(1)}, f32[1,32,64,256]{3,2,1,0:T(8,128)S(1)}, s32[]{:T(128)}, ...), condition=%wide.region_6.7_spmd.clone, body=%wide.region_5.6_spmd.clone.sunk | while | flops 2621443 | bytes 12583159 | solution.py:107
  131.9 12.0 %collective-permute-done = bf16[1,32,64,256]{3,2,1,0:T(8,128)(2,1)S(1)} collective-permute-done((bf16[1,32,64,256]{3,2,1,0:T(8,128)(2,1)}, bf16[1,32,64,256]{3,2,1,0:T(8,128)(2,1)S(1)}, u32[]{:S(2)}, u32[]{:S(2)}) %collective-permute-start) | collective-permute-done | bytes 1048608 | tf_op jit(solution)/shard_map/while/body/eval_jaxpr/ppermute | solution.py:17
  148.3 5.8 collective-permute-start
  154.1 12.0 %collective-permute-done = bf16[1,32,64,256]{3,2,1,0:T(8,128)(2,1)S(1)} collective-permute-done((bf16[1,32,64,256]{3,2,1,0:T(8,128)(2,1)}, bf16[1,32,64,256]{3,2,1,0:T(8,128)(2,1)S(1)}, u32[]{:S(2)}, u32[]{:S(2)}) %collective-permute-start) | collective-permute-done | bytes 1048608 | tf_op jit(solution)/shard_map/while/body/eval_jaxpr/ppermute | solution.py:17
  170.6 5.8 collective-permute-start
  176.3 12.0 %collective-permute-done = bf16[1,32,64,256]{3,2,1,0:T(8,128)(2,1)S(1)} collective-permute-done((bf16[1,32,64,256]{3,2,1,0:T(8,128)(2,1)}, bf16[1,32,64,256]{3,2,1,0:T(8,128)(2,1)S(1)}, u32[]{:S(2)}, u32[]{:S(2)}) %collective-permute-start) | collective-permute-done | bytes 1048608 | tf_op jit(solution)/shard_map/while/body/eval_jaxpr/ppermute | solution.py:17
  198.6 12.0 %collective-permute-done = bf16[1,32,64,256]{3,2,1,0:T(8,128)(2,1)S(1)} collective-permute-done((bf16[1,32,64,256]{3,2,1,0:T(8,128)(2,1)}, bf16[1,32,64,256]{3,2,1,0:T(8,128)(2,1)S(1)}, u32[]{:S(2)}, u32[]{:S(2)}) %collective-permute-start) | collective-permute-done | bytes 1048608 | tf_op jit(solution)/shard_map/while/body/eval_jaxpr/ppermute | solution.py:17
  220.8 12.0 %collective-permute-done = bf16[1,32,64,256]{3,2,1,0:T(8,128)(2,1)S(1)} collective-permute-done((bf16[1,32,64,256]{3,2,1,0:T(8,128)(2,1)}, bf16[1,32,64,256]{3,2,1,0:T(8,128)(2,1)S(1)}, u32[]{:S(2)}, u32[]{:S(2)}) %collective-permute-start) | collective-permute-done | bytes 1048608 | tf_op jit(solution)/shard_map/while/body/eval_jaxpr/ppermute | solution.py:17
  243.0 12.0 %collective-permute-done = bf16[1,32,64,256]{3,2,1,0:T(8,128)(2,1)S(1)} collective-permute-done((bf16[1,32,64,256]{3,2,1,0:T(8,128)(2,1)}, bf16[1,32,64,256]{3,2,1,0:T(8,128)(2,1)S(1)}, u32[]{:S(2)}, u32[]{:S(2)}) %collective-permute-start) | collective-permute-done | bytes 1048608 | tf_op jit(solution)/shard_map/while/body/eval_jaxpr/ppermute | solution.py:17
  259.4 5.8 collective-permute-start
  265.2 12.0 %collective-permute-done = bf16[1,32,64,256]{3,2,1,0:T(8,128)(2,1)S(1)} collective-permute-done((bf16[1,32,64,256]{3,2,1,0:T(8,128)(2,1)}, bf16[1,32,64,256]{3,2,1,0:T(8,128)(2,1)S(1)}, u32[]{:S(2)}, u32[]{:S(2)}) %collective-permute-start) | collective-permute-done | bytes 1048608 | tf_op jit(solution)/shard_map/while/body/eval_jaxpr/ppermute | solution.py:17
  287.4 12.0 %collective-permute-done = bf16[1,32,64,256]{3,2,1,0:T(8,128)(2,1)S(1)} collective-permute-done((bf16[1,32,64,256]{3,2,1,0:T(8,128)(2,1)}, bf16[1,32,64,256]{3,2,1,0:T(8,128)(2,1)S(1)}, u32[]{:S(2)}, u32[]{:S(2)}) %collective-permute-start) | collective-permute-done | bytes 1048608 | tf_op jit(solution)/shard_map/while/body/eval_jaxpr/ppermute | solution.py:17
  309.6 12.0 %collective-permute-done = bf16[1,32,64,256]{3,2,1,0:T(8,128)(2,1)S(1)} collective-permute-done((bf16[1,32,64,256]{3,2,1,0:T(8,128)(2,1)}, bf16[1,32,64,256]{3,2,1,0:T(8,128)(2,1)S(1)}, u32[]{:S(2)}, u32[]{:S(2)}) %collective-permute-start) | collective-permute-done | bytes 1048608 | tf_op jit(solution)/shard_map/while/body/eval_jaxpr/ppermute | solution.py:17
  331.8 12.0 %collective-permute-done = bf16[1,32,64,256]{3,2,1,0:T(8,128)(2,1)S(1)} collective-permute-done((bf16[1,32,64,256]{3,2,1,0:T(8,128)(2,1)}, bf16[1,32,64,256]{3,2,1,0:T(8,128)(2,1)S(1)}, u32[]{:S(2)}, u32[]{:S(2)}) %collective-permute-start) | collective-permute-done | bytes 1048608 | tf_op jit(solution)/shard_map/while/body/eval_jaxpr/ppermute | solution.py:17
  354.0 12.0 %collective-permute-done = bf16[1,32,64,256]{3,2,1,0:T(8,128)(2,1)S(1)} collective-permute-done((bf16[1,32,64,256]{3,2,1,0:T(8,128)(2,1)}, bf16[1,32,64,256]{3,2,1,0:T(8,128)(2,1)S(1)}, u32[]{:S(2)}, u32[]{:S(2)}) %collective-permute-start) | collective-permute-done | bytes 1048608 | tf_op jit(solution)/shard_map/while/body/eval_jaxpr/ppermute | solution.py:17
  376.3 12.0 %collective-permute-done = bf16[1,32,64,256]{3,2,1,0:T(8,128)(2,1)S(1)} collective-permute-done((bf16[1,32,64,256]{3,2,1,0:T(8,128)(2,1)}, bf16[1,32,64,256]{3,2,1,0:T(8,128)(2,1)S(1)}, u32[]{:S(2)}, u32[]{:S(2)}) %collective-permute-start) | collective-permute-done | bytes 1048608 | tf_op jit(solution)/shard_map/while/body/eval_jaxpr/ppermute | solution.py:17
  398.5 12.0 %collective-permute-done = bf16[1,32,64,256]{3,2,1,0:T(8,128)(2,1)S(1)} collective-permute-done((bf16[1,32,64,256]{3,2,1,0:T(8,128)(2,1)}, bf16[1,32,64,256]{3,2,1,0:T(8,128)(2,1)S(1)}, u32[]{:S(2)}, u32[]{:S(2)}) %collective-permute-start) | collective-permute-done | bytes 1048608 | tf_op jit(solution)/shard_map/while/body/eval_jaxpr/ppermute | solution.py:17
  414.9 5.8 collective-permute-start
  420.7 12.0 %collective-permute-done = bf16[1,32,64,256]{3,2,1,0:T(8,128)(2,1)S(1)} collective-permute-done((bf16[1,32,64,256]{3,2,1,0:T(8,128)(2,1)}, bf16[1,32,64,256]{3,2,1,0:T(8,128)(2,1)S(1)}, u32[]{:S(2)}, u32[]{:S(2)}) %collective-permute-start) | collective-permute-done | bytes 1048608 | tf_op jit(solution)/shard_map/while/body/eval_jaxpr/ppermute | solution.py:17
  442.9 12.0 %collective-permute-done = bf16[1,32,64,256]{3,2,1,0:T(8,128)(2,1)S(1)} collective-permute-done((bf16[1,32,64,256]{3,2,1,0:T(8,128)(2,1)}, bf16[1,32,64,256]{3,2,1,0:T(8,128)(2,1)S(1)}, u32[]{:S(2)}, u32[]{:S(2)}) %collective-permute-start) | collective-permute-done | bytes 1048608 | tf_op jit(solution)/shard_map/while/body/eval_jaxpr/ppermute | solution.py:17
  456.5 12.2 %fusion.9 = f32[8,32,64,128]{3,2,1,0:T(8,128)} fusion(bf16[8,128,256,1]{2,1,3,0:T(8,128)(2,1)} %bitcast.138, f32[8,1,32,64,256]{4,3,2,1,0:T(8,128)} %get-tuple-element.55, f32[32,64,256]{2,1,0:T(8,128)} %bitcast.130, f32[8,32]{1,0:T(8,128)S(1)} %copy-done.11), kind=kOutput, calls=%fused_computation.18 | convolution fusion | flops 1086324736 | bytes 27788288 | tf_op jit(solution)/shard_map/ctgn,cghpn->ctghp/dot_general | solution.py:110
  468.7 13.2 %fusion.16 = f32[8,128,1,32,64]{1,4,3,0,2:T(8,128)S(1)} fusion(f32[8,32,64,128]{3,2,1,0:T(8,128)} %fusion.9, f32[8,128,1,32,64]{1,0,4,3,2:T(8,128)} %bitcast.136, f32[32]{0:T(128)S(1)} %copy-done.25, f32[8,128,32]{1,2,0:T(8,128)S(1)} %copy-done.7, f32[8,32,128]{2,1,0:T(8,128)S(1)} %bitcast.146, f32[8,32,128]{2,1,0:T(8,128)S(1)} %bitcast.141, ...), kind=kOutput, calls=%fused_computation.29 | convolution fusion | flops 570425344 | bytes 30294144 | tf_op jit(solution)/shard_map/cghts,csghp->ctghp/dot_general | solution.py:83
  481.9 7.7 %copy.29 = f32[8,128,1,32,64]{1,0,4,3,2:T(8,128)S(1)} copy(f32[8,128,1,32,64]{1,4,3,0,2:T(8,128)S(1)} %fusion.16) | data formatting | bytes 16777216 | tf_op jit(solution)/shard_map/add | solution.py:114
  496.9 32.9 %convolution_convert_fusion = bf16[1024,4096]{1,0:T(8,128)(2,1)} fusion(bf16[2048,4096]{1,0:T(8,128)(2,1)} %param.29, f32[2048]{0:T(1024)S(1)} %copy-done.24, f32[1024]{0:T(1024)S(1)} %add_rsqrt_fusion, bf16[1024,2048]{0,1:T(8,128)(2,1)} %copy.30, f32[256,8,8,128]{3,2,1,0:T(8,128)} %bitcast.132), kind=kOutput, calls=%fused_computation.44 | convolution fusion | flops 17202937856 | bytes 37761024 | tf_op jit(solution)/shard_map/dot_general | solution.py:126
  529.8 184.5 %reduce-scatter.2.cloned.1.call-done = bf16[128,4096]{1,0:T(8,128)(2,1)} async-done(((bf16[1024,4096]{1,0:T(8,128)(2,1)}), bf16[128,4096]{1,0:T(8,128)(2,1)}) %reduce-scatter.2.cloned.1.call-update) | async-done | bytes 1048592 | tf_op jit(solution)/shard_map/reduce_scatter | solution.py:125
  (155 shorter events, 195.6 us)
Async XLA Ops:
  6.5 707.7 %reduce-scatter.2.cloned.1.call-start = ((), (), s32[]{:S(2)}) async-start(), calls=%async_computation.1 | async-start | bytes 9437184 | tf_op jit(solution)/shard_map/reduce_scatter | solution.py:125
  7.8 35.9 %collective-permute-start.2 = (bf16[2,3,256]{2,1,0:T(4,128)(2,1)}, bf16[2,3,256]{2,1,0:T(4,128)(2,1)}, u32[]{:S(2)}, u32[]{:S(2)}) collective-permute-start(bf16[2,3,256]{2,1,0:T(4,128)(2,1)} %slice.129), channel_id=1, source_target_pairs={{0,8},{8,16},{16,24},{24,32},{32,40},{40,48},{48,56},{56,64},{64,7... | collective-permute-start | bytes 9224 | tf_op jit(solution)/shard_map/ppermute | solution.py:17
  15.7 31.7 %collective-permute-start.1 = (bf16[3,2048]{0,1:T(8,128)(2,1)}, bf16[3,2048]{0,1:T(8,128)(2,1)}, u32[]{:S(2)}, u32[]{:S(2)}) collective-permute-start(bf16[3,2048]{0,1:T(8,128)(2,1)} %copy.19), channel_id=1, source_target_pairs={{0,8},{8,16},{16,24},{24,32},{32,40},{40,48},{48,56},{56,64},{64,7... | collective-permute-start | bytes 36872 | tf_op jit(solution)/shard_map/ppermute | solution.py:17
  37.3 8.2 %copy-start.14 = (f32[1,1,256]{2,1,0:T(1,128)S(1)}, f32[1,1,256]{2,1,0:T(1,128)}, u32[]{:S(2)}) copy-start(f32[1,1,256]{2,1,0:T(1,128)} %get-tuple-element.136) | copy-start | bytes 3076
  37.3 8.2 %copy-start.15 = (f32[1,1,256]{2,1,0:T(1,128)S(1)}, f32[1,1,256]{2,1,0:T(1,128)}, u32[]{:S(2)}) copy-start(f32[1,1,256]{2,1,0:T(1,128)} %get-tuple-element.137) | copy-start | bytes 3076
  37.3 8.2 %copy-start.16 = (f32[1,1,256]{2,1,0:T(1,128)S(1)}, f32[1,1,256]{2,1,0:T(1,128)}, u32[]{:S(2)}) copy-start(f32[1,1,256]{2,1,0:T(1,128)} %get-tuple-element.138) | copy-start | bytes 3076
  37.3 8.2 %copy-start.17 = (f32[1,1,256]{2,1,0:T(1,128)S(1)}, f32[1,1,256]{2,1,0:T(1,128)}, u32[]{:S(2)}) copy-start(f32[1,1,256]{2,1,0:T(1,128)} %get-tuple-element.139) | copy-start | bytes 3076
  37.3 8.2 %copy-start.22 = (f32[1,256]{1,0:T(1,128)S(1)}, f32[1,256]{1,0:T(1,128)}, u32[]{:S(2)}) copy-start(f32[1,256]{1,0:T(1,128)} %get-tuple-element.145) | copy-start | bytes 3076
  46.3 14.7 %copy-start.4 = (bf16[1024,256]{1,0:T(8,128)(2,1)}, bf16[1024,256]{1,0:T(8,128)(2,1)S(1)}, u32[]{:S(2)}) copy-start(bf16[1024,256]{1,0:T(8,128)(2,1)S(1)} %multiply_convert_fusion.9) | copy-start | bytes 1572868
  118.1 8.7 %copy-start.10 = (f32[32]{0:T(128)S(1)}, f32[32]{0:T(128)}, u32[]{:S(2)}) copy-start(f32[32]{0:T(128)} %get-tuple-element.101) | copy-start | bytes 388
  126.8 329.7 %copy-start.11 = (f32[8,32]{1,0:T(8,128)S(1)}, f32[8,32]{1,0:T(8,128)}, u32[]{:S(2)}) copy-start(f32[8,32]{1,0:T(8,128)} %subtract_exponential_fusion) | copy-start | bytes 3076
  128.1 15.9 %collective-permute-start = (bf16[1,32,64,256]{3,2,1,0:T(8,128)(2,1)}, bf16[1,32,64,256]{3,2,1,0:T(8,128)(2,1)S(1)}, u32[]{:S(2)}, u32[]{:S(2)}) collective-permute-start(bf16[1,32,64,256]{3,2,1,0:T(8,128)(2,1)} %fusion.57), channel_id=1, source_target_pairs={{0,8},{8,16},{16,24},{24,32},{32,40},{40,48},{48,56},{56,64},{64,7... | collective-permute-start | bytes 3145736 | tf_op jit(solution)/shard_map/while/body/eval_jaxpr/ppermute | solution.py:17
  148.3 17.8 %collective-permute-start = (bf16[1,32,64,256]{3,2,1,0:T(8,128)(2,1)}, bf16[1,32,64,256]{3,2,1,0:T(8,128)(2,1)S(1)}, u32[]{:S(2)}, u32[]{:S(2)}) collective-permute-start(bf16[1,32,64,256]{3,2,1,0:T(8,128)(2,1)} %fusion.57), channel_id=1, source_target_pairs={{0,8},{8,16},{16,24},{24,32},{32,40},{40,48},{48,56},{56,64},{64,7... | collective-permute-start | bytes 3145736 | tf_op jit(solution)/shard_map/while/body/eval_jaxpr/ppermute | solution.py:17
  170.6 17.8 %collective-permute-start = (bf16[1,32,64,256]{3,2,1,0:T(8,128)(2,1)}, bf16[1,32,64,256]{3,2,1,0:T(8,128)(2,1)S(1)}, u32[]{:S(2)}, u32[]{:S(2)}) collective-permute-start(bf16[1,32,64,256]{3,2,1,0:T(8,128)(2,1)} %fusion.57), channel_id=1, source_target_pairs={{0,8},{8,16},{16,24},{24,32},{32,40},{40,48},{48,56},{56,64},{64,7... | collective-permute-start | bytes 3145736 | tf_op jit(solution)/shard_map/while/body/eval_jaxpr/ppermute | solution.py:17
  192.8 17.8 %collective-permute-start = (bf16[1,32,64,256]{3,2,1,0:T(8,128)(2,1)}, bf16[1,32,64,256]{3,2,1,0:T(8,128)(2,1)S(1)}, u32[]{:S(2)}, u32[]{:S(2)}) collective-permute-start(bf16[1,32,64,256]{3,2,1,0:T(8,128)(2,1)} %fusion.57), channel_id=1, source_target_pairs={{0,8},{8,16},{16,24},{24,32},{32,40},{40,48},{48,56},{56,64},{64,7... | collective-permute-start | bytes 3145736 | tf_op jit(solution)/shard_map/while/body/eval_jaxpr/ppermute | solution.py:17
  215.0 17.8 %collective-permute-start = (bf16[1,32,64,256]{3,2,1,0:T(8,128)(2,1)}, bf16[1,32,64,256]{3,2,1,0:T(8,128)(2,1)S(1)}, u32[]{:S(2)}, u32[]{:S(2)}) collective-permute-start(bf16[1,32,64,256]{3,2,1,0:T(8,128)(2,1)} %fusion.57), channel_id=1, source_target_pairs={{0,8},{8,16},{16,24},{24,32},{32,40},{40,48},{48,56},{56,64},{64,7... | collective-permute-start | bytes 3145736 | tf_op jit(solution)/shard_map/while/body/eval_jaxpr/ppermute | solution.py:17
  237.2 17.8 %collective-permute-start = (bf16[1,32,64,256]{3,2,1,0:T(8,128)(2,1)}, bf16[1,32,64,256]{3,2,1,0:T(8,128)(2,1)S(1)}, u32[]{:S(2)}, u32[]{:S(2)}) collective-permute-start(bf16[1,32,64,256]{3,2,1,0:T(8,128)(2,1)} %fusion.57), channel_id=1, source_target_pairs={{0,8},{8,16},{16,24},{24,32},{32,40},{40,48},{48,56},{56,64},{64,7... | collective-permute-start | bytes 3145736 | tf_op jit(solution)/shard_map/while/body/eval_jaxpr/ppermute | solution.py:17
  259.4 17.8 %collective-permute-start = (bf16[1,32,64,256]{3,2,1,0:T(8,128)(2,1)}, bf16[1,32,64,256]{3,2,1,0:T(8,128)(2,1)S(1)}, u32[]{:S(2)}, u32[]{:S(2)}) collective-permute-start(bf16[1,32,64,256]{3,2,1,0:T(8,128)(2,1)} %fusion.57), channel_id=1, source_target_pairs={{0,8},{8,16},{16,24},{24,32},{32,40},{40,48},{48,56},{56,64},{64,7... | collective-permute-start | bytes 3145736 | tf_op jit(solution)/shard_map/while/body/eval_jaxpr/ppermute | solution.py:17
  281.6 17.8 %collective-permute-start = (bf16[1,32,64,256]{3,2,1,0:T(8,128)(2,1)}, bf16[1,32,64,256]{3,2,1,0:T(8,128)(2,1)S(1)}, u32[]{:S(2)}, u32[]{:S(2)}) collective-permute-start(bf16[1,32,64,256]{3,2,1,0:T(8,128)(2,1)} %fusion.57), channel_id=1, source_target_pairs={{0,8},{8,16},{16,24},{24,32},{32,40},{40,48},{48,56},{56,64},{64,7... | collective-permute-start | bytes 3145736 | tf_op jit(solution)/shard_map/while/body/eval_jaxpr/ppermute | solution.py:17
  303.8 17.8 %collective-permute-start = (bf16[1,32,64,256]{3,2,1,0:T(8,128)(2,1)}, bf16[1,32,64,256]{3,2,1,0:T(8,128)(2,1)S(1)}, u32[]{:S(2)}, u32[]{:S(2)}) collective-permute-start(bf16[1,32,64,256]{3,2,1,0:T(8,128)(2,1)} %fusion.57), channel_id=1, source_target_pairs={{0,8},{8,16},{16,24},{24,32},{32,40},{40,48},{48,56},{56,64},{64,7... | collective-permute-start | bytes 3145736 | tf_op jit(solution)/shard_map/while/body/eval_jaxpr/ppermute | solution.py:17
  326.0 17.8 %collective-permute-start = (bf16[1,32,64,256]{3,2,1,0:T(8,128)(2,1)}, bf16[1,32,64,256]{3,2,1,0:T(8,128)(2,1)S(1)}, u32[]{:S(2)}, u32[]{:S(2)}) collective-permute-start(bf16[1,32,64,256]{3,2,1,0:T(8,128)(2,1)} %fusion.57), channel_id=1, source_target_pairs={{0,8},{8,16},{16,24},{24,32},{32,40},{40,48},{48,56},{56,64},{64,7... | collective-permute-start | bytes 3145736 | tf_op jit(solution)/shard_map/while/body/eval_jaxpr/ppermute | solution.py:17
  348.3 17.8 %collective-permute-start = (bf16[1,32,64,256]{3,2,1,0:T(8,128)(2,1)}, bf16[1,32,64,256]{3,2,1,0:T(8,128)(2,1)S(1)}, u32[]{:S(2)}, u32[]{:S(2)}) collective-permute-start(bf16[1,32,64,256]{3,2,1,0:T(8,128)(2,1)} %fusion.57), channel_id=1, source_target_pairs={{0,8},{8,16},{16,24},{24,32},{32,40},{40,48},{48,56},{56,64},{64,7... | collective-permute-start | bytes 3145736 | tf_op jit(solution)/shard_map/while/body/eval_jaxpr/ppermute | solution.py:17
  370.5 17.8 %collective-permute-start = (bf16[1,32,64,256]{3,2,1,0:T(8,128)(2,1)}, bf16[1,32,64,256]{3,2,1,0:T(8,128)(2,1)S(1)}, u32[]{:S(2)}, u32[]{:S(2)}) collective-permute-start(bf16[1,32,64,256]{3,2,1,0:T(8,128)(2,1)} %fusion.57), channel_id=1, source_target_pairs={{0,8},{8,16},{16,24},{24,32},{32,40},{40,48},{48,56},{56,64},{64,7... | collective-permute-start | bytes 3145736 | tf_op jit(solution)/shard_map/while/body/eval_jaxpr/ppermute | solution.py:17
  392.7 17.8 %collective-permute-start = (bf16[1,32,64,256]{3,2,1,0:T(8,128)(2,1)}, bf16[1,32,64,256]{3,2,1,0:T(8,128)(2,1)S(1)}, u32[]{:S(2)}, u32[]{:S(2)}) collective-permute-start(bf16[1,32,64,256]{3,2,1,0:T(8,128)(2,1)} %fusion.57), channel_id=1, source_target_pairs={{0,8},{8,16},{16,24},{24,32},{32,40},{40,48},{48,56},{56,64},{64,7... | collective-permute-start | bytes 3145736 | tf_op jit(solution)/shard_map/while/body/eval_jaxpr/ppermute | solution.py:17
  414.9 17.8 %collective-permute-start = (bf16[1,32,64,256]{3,2,1,0:T(8,128)(2,1)}, bf16[1,32,64,256]{3,2,1,0:T(8,128)(2,1)S(1)}, u32[]{:S(2)}, u32[]{:S(2)}) collective-permute-start(bf16[1,32,64,256]{3,2,1,0:T(8,128)(2,1)} %fusion.57), channel_id=1, source_target_pairs={{0,8},{8,16},{16,24},{24,32},{32,40},{40,48},{48,56},{56,64},{64,7... | collective-permute-start | bytes 3145736 | tf_op jit(solution)/shard_map/while/body/eval_jaxpr/ppermute | solution.py:17
  437.1 17.8 %collective-permute-start = (bf16[1,32,64,256]{3,2,1,0:T(8,128)(2,1)}, bf16[1,32,64,256]{3,2,1,0:T(8,128)(2,1)S(1)}, u32[]{:S(2)}, u32[]{:S(2)}) collective-permute-start(bf16[1,32,64,256]{3,2,1,0:T(8,128)(2,1)} %fusion.57), channel_id=1, source_target_pairs={{0,8},{8,16},{16,24},{24,32},{32,40},{40,48},{48,56},{56,64},{64,7... | collective-permute-start | bytes 3145736 | tf_op jit(solution)/shard_map/while/body/eval_jaxpr/ppermute | solution.py:17
  456.5 12.2 %copy-start.5 = (f32[8,128,128]{2,1,0:T(8,128)S(1)}, f32[8,128,128]{2,1,0:T(8,128)}, u32[]{:S(2)}) copy-start(f32[8,128,128]{2,1,0:T(8,128)} %fusion.48) | copy-start | bytes 1572868
  456.5 12.2 %copy-start.6 = (f32[8,128,1,32]{1,3,2,0:T(8,128)S(1)}, f32[8,128,1,32]{1,3,2,0:T(8,128)}, u32[]{:S(2)}) copy-start(f32[8,128,1,32]{1,3,2,0:T(8,128)} %copy.57) | copy-start | bytes 393220
  456.5 12.2 %copy-start.7 = (f32[8,128,32]{1,2,0:T(8,128)S(1)}, f32[8,128,32]{1,2,0:T(8,128)}, u32[]{:S(2)}) copy-start(f32[8,128,32]{1,2,0:T(8,128)} %get-tuple-element.126) | copy-start | bytes 393220
  456.5 12.2 %copy-start.12 = (pred[128,128]{1,0:T(8,128)(4,1)S(1)}, pred[128,128]{1,0:T(8,128)(4,1)}, u32[]{:S(2)}) copy-start(pred[128,128]{1,0:T(8,128)(4,1)} %iota_compare_fusion) | copy-start | bytes 49156
  456.5 12.2 %copy-start.25 = (f32[32]{0:T(128)S(1)}, f32[32]{0:T(128)}, u32[]{:S(2)}) copy-start(f32[32]{0:T(128)} %param.27) | copy-start | bytes 388
  481.9 11.0 %copy-start.2 = (bf16[1024,2048]{0,1:T(8,128)(2,1)S(1)}, bf16[1024,2048]{0,1:T(8,128)(2,1)}, u32[]{:S(2)}) copy-start(bf16[1024,2048]{0,1:T(8,128)(2,1)} %copy.30) | copy-start | bytes 12582916
  (12 other events, 67.3 us)
Sparse Core Ops, SparseCore 0:
  529.9 184.3 reduce-scatter.1
where the time goes:
time: 733 us; the launch traced here: 722 us
  waiting for transfers between devices  365 us (50%)
  other arithmetic  119 us (16%)
  starting transfers between devices  92.7 us (13%)
  matrix products  67.4 us (9%)
  local copies, waits for them, and re-layouts  51.1 us (7%)
  between operations  14.2 us (2%)
  loops' own time  11.8 us (2%)
    reduce_scatter x1, waiting for transfers between devices, per_device(): lax.psum_scatter(jnp.dot(normed, out_weight, preferred_element_type=jnp.f...  185 us
    ppermute x17, waiting for transfers between devices, shifted(): return lax.ppermute(value, axis, pairs)  181 us
    ppermute x17, starting transfers between devices, shifted(): return lax.ppermute(value, axis, pairs)  92.7 us
    convert_element_type x30, other arithmetic, pass_on(): return shifted(leaving.astype(jnp.bfloat16), 'seq', 1).astype(leaving.dtype)  64.3 us
    dot_general x1, matrix products, per_device(): jnp.dot(normed, out_weight, preferred_element_type=jnp.float32)  32.9 us
    unnamed x58, local copies, waits for them, and re-layouts  27.9 us
    add x8, other arithmetic, advance(): return (decay[..., None, None] * carry + state, carry)  15.7 us
  transfers between devices with their start and end apart: 18, of which 16 were waited for; matrix products, arithmetic and copies ran while one was open for 4% of the time, Pallas kernels for 0%

commit v1 on v0

v1 whole, which is shorter than its diff:
```python
import functools

import jax
import jax.numpy as jnp
from jax import lax
from jax.experimental import pallas as pl
from jax.experimental.pallas import tpu as pltpu
from jax.sharding import PartitionSpec as P

H = 256
P_SIZE = 64
N = 256
G = 8
KW = 4
BLOCK = 128
MESH = pl.DeviceIdType.MESH


def shifted(value, axis, by):
    devices = lax.axis_size(axis)
    pairs = [(i, i + by) for i in range(devices) if 0 <= i + by < devices]
    return lax.ppermute(value, axis, pairs)


CHUNKS = 4
TILE = 256


def project_kernel(rows, normed_ref, weight_ref, out_ref, w, sent, got, kept, xsent, xgot,
                   wsem, send_sem, recv_sem, xsend_sem, xrecv_sem):
    head = lax.axis_index("head")
    y = head // 2
    x = lax.rem(head, 2)
    wide = out_ref.shape[1] // CHUNKS
    up = {"head": lax.rem(y + 1, 4) * 2 + x}
    down = {"head": lax.rem(y + 3, 4) * 2 + x}
    across = {"head": y * 2 + 1 - x}
    loads = []
    for c in range(CHUNKS):
        load = pltpu.make_async_copy(
            weight_ref.at[:, c * wide : (c + 1) * wide], w.at[c], wsem.at[c]
        )
        load.start()
        loads.append(load)
    barrier = pltpu.get_barrier_semaphore()
    for to in (up, down, across):
        pl.semaphore_signal(barrier, inc=1, device_id=to, device_id_type=MESH)
    pl.semaphore_wait(barrier, 3)

    def ring(c, s, role):
        return pltpu.make_async_remote_copy(
            src_ref=sent.at[c, s, role],
            dst_ref=got.at[c, s, role],
            send_sem=send_sem.at[c, s, role],
            recv_sem=recv_sem.at[c, s, role],
            device_id=up if role == 0 else down,
            device_id_type=MESH,
        )

    def cross(c):
        return pltpu.make_async_remote_copy(
            src_ref=xsent.at[c],
            dst_ref=xgot.at[c],
            send_sem=xsend_sem.at[c],
            recv_sem=xrecv_sem.at[c],
            device_id=across,
            device_id_type=MESH,
        )

    def event(c, s):
        if s == 0:
            if loads[c] is not None:
                loads[c].wait()
        else:
            for role in (0, 1):
                ring(c, s - 1, role).wait_recv()
        block0 = lax.rem(y + 3 - s, 4) * 2 + 1 - x
        block1 = lax.rem(y + 1 + s, 4) * 2 + x
        row0 = pl.multiple_of(block0 * rows, rows)
        row1 = pl.multiple_of(block1 * rows, rows)

        @pl.loop(0, wide // TILE)
        def _(t):
            cols = pl.ds(pl.multiple_of(t * TILE, TILE), TILE)
            left = jnp.concatenate(
                [normed_ref[pl.ds(row0, rows), :], normed_ref[pl.ds(row1, rows), :]], axis=0
            )
            part = jnp.dot(left, w[c, :, cols], preferred_element_type=jnp.float32)
            part0, part1 = part[:rows], part[rows:]
            if s > 0:
                part0 = part0 + got[c, s - 1, 0, :, cols].astype(jnp.float32)
                part1 = part1 + got[c, s - 1, 1, :, cols].astype(jnp.float32)
            if s < 3:
                sent[c, s, 0, :, cols] = part0.astype(jnp.bfloat16)
                sent[c, s, 1, :, cols] = part1.astype(jnp.bfloat16)
            else:
                xsent[c, :, cols] = part0.astype(jnp.bfloat16)
                kept[c, :, cols] = part1

        if s < 3:
            ring(c, s, 0).start()
            ring(c, s, 1).start()
        else:
            cross(c).start()

    def finish(c):
        cross(c).wait_recv()
        out_ref[:, c * wide : (c + 1) * wide] = (
            kept[c] + xgot[c].astype(jnp.float32)
        ).astype(jnp.bfloat16)

    for c, s in ((0, 0), (1, 0), (0, 1), (1, 1), (0, 2), (1, 2), (2, 0), (0, 3), (3, 0), (1, 3),
                 (2, 1), (3, 1), (2, 2), (3, 2), (2, 3), (3, 3)):
        event(c, s)
        if s == 3 and c >= 2:
            finish(c - 2)
    finish(2)
    finish(3)
    for c in range(CHUNKS):
        cross(c).wait_send()
        for s in range(3):
            for role in (0, 1):
                ring(c, s, role).wait_send()


def project(normed, weight):
    tokens, depth = normed.shape
    width = weight.shape[1]
    rows = tokens // 8
    wide = width // CHUNKS
    dma = pltpu.SemaphoreType.DMA
    return pl.pallas_call(
        functools.partial(project_kernel, rows),
        out_shape=jax.ShapeDtypeStruct((rows, width), jnp.bfloat16),
        in_specs=[pl.BlockSpec(memory_space=pltpu.VMEM), pl.BlockSpec(memory_space=pl.ANY)],
        out_specs=pl.BlockSpec(memory_space=pltpu.VMEM),
        scratch_shapes=[
            pltpu.VMEM((CHUNKS, depth, wide), jnp.bfloat16),
            pltpu.VMEM((CHUNKS, 3, 2, rows, wide), jnp.bfloat16),
            pltpu.VMEM((CHUNKS, 3, 2, rows, wide), jnp.bfloat16),
            pltpu.VMEM((CHUNKS, rows, wide), jnp.float32),
            pltpu.VMEM((CHUNKS, rows, wide), jnp.bfloat16),
            pltpu.VMEM((CHUNKS, rows, wide), jnp.bfloat16),
            dma((CHUNKS,)),
            dma((CHUNKS, 3, 2)),
            dma((CHUNKS, 3, 2)),
            dma((CHUNKS,)),
            dma((CHUNKS,)),
        ],
        compiler_params=pltpu.CompilerParams(
            collective_id=1, has_side_effects=True, vmem_limit_bytes=60 * 1024 * 1024
        ),
        name="project",
    )(normed, weight)


def conv_silu(extended, weight, bias, length):
    padded = extended.astype(jnp.float32)
    total = jnp.zeros((length, extended.shape[1]), jnp.float32) + bias[None, :]
    for offset in range(KW):
        total = total + weight[offset][None, :] * padded[offset : offset + length]
    return jax.nn.silu(total).astype(jnp.bfloat16)


def per_device(
    x_values,
    bc_values,
    z_values,
    dt_values,
    xconv_weight,
    bconv_weight,
    xconv_bias,
    bconv_bias,
    dt_offset,
    decay_log,
    skip_gain,
    norm_gain,
    out_weight,
):
    rows_here = x_values.shape[0]
    heads_here = dt_values.shape[1]
    blocks = rows_here // BLOCK
    margin = KW - 1
    prev_x, prev_bc = shifted(
        (x_values[rows_here - margin :], bc_values[:, rows_here - margin :]), "seq", 1
    )
    x_conv = conv_silu(
        jnp.concatenate([prev_x, x_values], axis=0), xconv_weight, xconv_bias, rows_here
    )
    b_conv = conv_silu(
        jnp.concatenate([prev_bc[0], bc_values[0]], axis=0),
        bconv_weight[0],
        bconv_bias[0],
        rows_here,
    )
    c_conv = conv_silu(
        jnp.concatenate([prev_bc[1], bc_values[1]], axis=0),
        bconv_weight[1],
        bconv_bias[1],
        rows_here,
    )
    steps_dt = jax.nn.softplus(dt_values.astype(jnp.float32) + dt_offset[None, :])
    log_decay = steps_dt * (-jnp.exp(decay_log))[None, :]
    x_blocks = x_conv.reshape(blocks, BLOCK, heads_here, P_SIZE)
    b_blocks = b_conv.reshape(blocks, BLOCK, N)
    c_blocks = c_conv.reshape(blocks, BLOCK, N)
    dt_blocks = jnp.transpose(steps_dt.reshape(blocks, BLOCK, heads_here), (0, 2, 1))
    cumul = jnp.cumsum(
        jnp.transpose(log_decay.reshape(blocks, BLOCK, heads_here), (0, 2, 1)), axis=2
    )
    positions = jnp.arange(BLOCK)
    causal = positions[:, None] >= positions[None, :]
    inner = jnp.einsum("ctn,csn->cts", c_blocks, b_blocks, preferred_element_type=jnp.float32)
    diff = cumul[..., :, None] - cumul[..., None, :]
    weights = jnp.where(causal, jnp.exp(jnp.where(causal, diff, 0.0)), 0.0)
    scores = (inner[:, None] * weights * dt_blocks[..., None, :]).astype(jnp.bfloat16)
    y_intra = jnp.einsum("chts,cshp->cthp", scores, x_blocks, preferred_element_type=jnp.float32)
    to_end = jnp.exp(cumul[..., -1:] - cumul) * dt_blocks
    x_weighted = (
        x_blocks.astype(jnp.float32) * jnp.transpose(to_end, (0, 2, 1))[..., None]
    ).astype(jnp.bfloat16)
    states = jnp.einsum("cshp,csn->chpn", x_weighted, b_blocks, preferred_element_type=jnp.float32)
    block_total = cumul[..., -1]
    block_decay = jnp.exp(block_total)
    carry = jnp.zeros((heads_here, P_SIZE, N), jnp.float32)
    local_before = []
    for c in range(blocks):
        local_before.append(carry)
        carry = block_decay[c][..., None, None] * carry + states[c]
    device_decay = jnp.exp(jnp.sum(block_total, axis=0))
    devices = lax.axis_size("seq")
    share = heads_here // devices
    ends = lax.all_to_all(
        carry.astype(jnp.bfloat16).reshape(devices, share, P_SIZE, N), "seq", 0, 0
    )
    decays = lax.all_to_all(device_decay.reshape(devices, share), "seq", 0, 0)
    run = jnp.zeros((share, P_SIZE, N), jnp.float32)
    prefix = []
    for i in range(devices):
        prefix.append(run.astype(jnp.bfloat16))
        run = decays[i][:, None, None] * run + ends[i].astype(jnp.float32)
    incoming = (
        lax.all_to_all(jnp.stack(prefix), "seq", 0, 0)
        .reshape(heads_here, P_SIZE, N)
        .astype(jnp.float32)
    )
    lead = jnp.cumsum(block_total, axis=0) - block_total
    before = (jnp.stack(local_before) + jnp.exp(lead)[..., None, None] * incoming[None]).astype(
        jnp.bfloat16
    )
    y_state = jnp.transpose(jnp.exp(cumul), (0, 2, 1))[..., None] * jnp.einsum(
        "ctn,chpn->cthp", c_blocks, before, preferred_element_type=jnp.float32
    )
    total = y_intra + y_state + skip_gain[None, None, :, None] * x_blocks.astype(jnp.float32)
    width = heads_here * P_SIZE
    gated = total.reshape(rows_here, width) * jax.nn.silu(z_values.astype(jnp.float32))
    scale = lax.rsqrt(jnp.mean(gated * gated, axis=1, keepdims=True) + 1e-05)
    normed = (gated * scale * norm_gain[None, :]).astype(jnp.bfloat16)
    return project(normed, out_weight)


def solution(mesh):
    return jax.shard_map(
        per_device,
        mesh=mesh,
        in_specs=(
            P("seq", "head"),
            P(None, "seq", "head"),
            P("seq", "head"),
            P("seq", "head"),
            P(None, "head"),
            P(None, None, "head"),
            P("head"),
            P(None, "head"),
            P("head"),
            P("head"),
            P("head"),
            P("head"),
            P("head", None),
        ),
        out_specs=P(("seq", "head"), None),
        check_vma=False,
    )
```

time: 733 us -> 308 us (0.42); the launches traced: 722 us -> 305 us
  waiting for transfers between devices: 365 us -> 12.6 us
  Pallas kernels: 0 us -> 86.4 us
  starting transfers between devices: 92.7 us -> 27 us
  other arithmetic: 119 us -> 74.8 us
  matrix products: 67.4 us -> 30.2 us
  local copies, waits for them, and re-layouts: 51.1 us -> 73.9 us
  between operations: 14.2 us -> 0.42 us
  loops' own time: 11.8 us -> 0 us
    reduce_scatter x1 -> x0, waiting for transfers between devices: 185 us -> none  [per_device(): lax.psum_scatter(jnp.dot(normed, out_weight, preferred_element_type=jnp.f...]
    ppermute x17 -> x2, waiting for transfers between devices: 181 us -> 0.01 us  [shifted(): return lax.ppermute(value, axis, pairs)]
    pallas_call x0 -> x1, Pallas kernels: none -> 86.4 us  [project(): pl.pallas_call(functools.partial(project_kernel, rows), out_shape=jax.Sha...]
    ppermute x17 -> x2, starting transfers between devices: 92.7 us -> 7.95 us  [shifted(): return lax.ppermute(value, axis, pairs)]
    reshape x2 -> x5, local copies, waits for them, and re-layouts: 0.7 us -> 55.4 us  [the longest x2 31.1 us: per_device(): total.reshape(rows_here, width) * jax.nn.silu(z_values.astype(jnp.float32))]
    convert_element_type x31 -> x3, other arithmetic: 65.6 us -> 13.1 us  [the longest x1 6.33 us: per_device(): carry.astype(jnp.bfloat16).reshape(devices, share, P_SIZE, N)]
    dot_general x5 -> x4, matrix products: 67.4 us -> 30.2 us  [the longest x1 12.6 us: per_device(): jnp.einsum('chts,cshp->cthp', scores, x_blocks, preferred_element_type=jn...]
    all_to_all x0 -> x3, starting transfers between devices: none -> 19 us  [the longest x1 7.23 us: per_device(): lax.all_to_all(carry.astype(jnp.bfloat16).reshape(devices, share, P_SIZE,...]
  transfers between devices with their start and end apart: 18 -> 5, of which waited for: 16 -> 2; matrix products, arithmetic and copies ran while one was open for 4% -> 13% of each run, Pallas kernels for 0% -> 0%
where the time goes in v1:
time: 308 us; the launch traced here: 305 us
  Pallas kernels  86.4 us (28%)
  other arithmetic  74.8 us (24%)
  local copies, waits for them, and re-layouts  73.9 us (24%)
  matrix products  30.2 us (10%)
  starting transfers between devices  27 us (9%)
  waiting for transfers between devices  12.6 us (4%)
    pallas_call x1, Pallas kernels, project(): pl.pallas_call(functools.partial(project_kernel, rows), out_shape=jax.Sha...  86.4 us
    reshape x2, local copies, waits for them, and re-layouts, per_device(): total.reshape(rows_here, width) * jax.nn.silu(z_values.astype(jnp.float32))  31.1 us
    unnamed x20, other arithmetic  29.8 us
    reshape x2, local copies, waits for them, and re-layouts, per_device(): x_blocks = x_conv.reshape(blocks, BLOCK, heads_here, P_SIZE)  24.4 us
    dot_general x1, matrix products, per_device(): jnp.einsum('chts,cshp->cthp', scores, x_blocks, preferred_element_type=jn...  12.6 us
    dot_general x1, matrix products, per_device(): jnp.einsum('ctn,chpn->cthp', c_blocks, before, preferred_element_type=jnp...  11.9 us
    unnamed x80, local copies, waits for them, and re-layouts  11.1 us
    convert_element_type x3, other arithmetic, conv_silu(): return jax.nn.silu(total).astype(jnp.bfloat16)  8.06 us
  transfers between devices with their start and end apart: 5, of which 2 were waited for; matrix products, arithmetic and copies ran while one was open for 13% of the time, Pallas kernels for 0%

profile of v1, /device:TPU:1, one launch (start us, length us, event | category | flops | bytes accessed | tf_op | source)
XLA Modules:
  0.0 305.2 jit_solution(15306181672715609640)
XLA Ops:
  0.8 6.0 %collective-permute-start.1 = (bf16[2,3,256]{2,1,0:T(4,128)(2,1)S(1)}, bf16[2,3,256]{2,1,0:T(4,128)(2,1)S(1)}, u32[]{:S(2)}, u32[]{:S(2)}) collective-permute-start(bf16[2,3,256]{2,1,0:T(4,128)(2,1)S(1)} %slice.282), channel_id=1, source_target_pairs={{0,8},{8,16},{16,24},{24,32},{32,40},{40,48},{48,56},{56,64},{64,7... | collective-permute-start | bytes 9224 | tf_op jit(solution)/shard_map/ppermute | solution.py:22
  7.6 1.9 collective-permute-start
  11.2 2.3 reduce_window_sum.22
  14.4 6.7 %all-to-all-start = ((f32[16,1,2]{2,1,0:T(1,128)}), f32[16,1,2]{2,1,0:T(1,128)S(1)}, u32[]{:S(2)}, u32[]{:S(2)}) async-start(f32[16,1,2]{2,1,0:T(1,128)} %bitcast.36), calls=%async_computation | async-start | bytes 16384 | tf_op jit(solution)/shard_map/all_to_all | solution.py:236
  21.1 1.3 slice_bitcast_fusion
  22.4 1.6 broadcast_dynamic-update-slice_fusion
  35.9 6.7 %multiply_convert_fusion.3 = bf16[1024,2048]{1,0:T(8,128)(2,1)} fusion(f32[1027,2048]{1,0:T(8,128)S(1)} %maximum_convert_fusion, f32[2048]{0:T(1024)S(1)} %bitcast.138, f32[2048]{0:T(1024)S(1)} %bitcast.139, f32[2048]{0:T(1024)S(1)} %bitcast.137, f32[2048]{0:T(1024)S(1)} %bitcast.136, f32[2048]{0:T(1024)S(1)} %copy-done.15), kind=kLoop, calls=%fused_computation.32 | loop fusion | flops 27262976 | bytes 37789696 | tf_op jit(solution)/shard_map/convert_element_type | solution.py:162
  42.6 12.9 %reshape.183 = bf16[8,128,32,64]{3,2,1,0:T(8,128)(2,1)} reshape(bf16[1024,2048]{1,0:T(8,128)(2,1)} %multiply_convert_fusion.3) | data formatting | bytes 8388608 | tf_op jit(solution)/shard_map/reshape | solution.py:204
  55.5 11.5 %copy.29 = bf16[8,128,32,64]{1,3,2,0:T(8,128)(2,1)} copy(bf16[8,128,32,64]{3,2,1,0:T(8,128)(2,1)} %reshape.183) | data formatting | bytes 8388608 | tf_op jit(solution)/shard_map/reshape | solution.py:204
  67.0 4.5 %fusion.20 = f32[8,32,64,256]{3,2,1,0:T(8,128)S(1)} fusion(bf16[8,128,256,1]{2,1,3,0:T(8,128)(2,1)S(1)} %bitcast.131, bf16[8,128,32,64]{1,3,2,0:T(8,128)(2,1)} %copy.29, f32[8,128,32]{1,2,0:T(8,128)S(1)} %bitcast_multiply_fusion), kind=kOutput, calls=%fused_computation.35 | convolution fusion | flops 1080033280 | bytes 21626880 | tf_op jit(solution)/shard_map/cshp,csn->chpn/dot_general | solution.py:222
  71.5 6.4 %fusion.56 = (f32[1,32,64,256]{3,2,1,0:T(8,128)S(1)}, f32[8,32,64,256]{3,2,1,0:T(8,128)}, f32[1,32,64,256]{3,2,1,0:T(8,128)S(1)}, f32[1,32,64,256]{3,2,1,0:T(8,1...) fusion(f32[8,32,64,256]{3,2,1,0:T(8,128)S(1)} %fusion.20, ...), kind=kLoop, calls=%fused_computation.161 | loop fusion | flops 524288 | bytes 35652096 | tf_op jit(solution)/shard_map/slice | solution.py:229
  77.9 3.7 %copy-done = f32[8,32,64,256]{3,2,1,0:T(8,128)} copy-done((f32[8,32,64,256]{3,2,1,0:T(8,128)}, f32[8,32,64,256]{3,2,1,0:T(8,128)S(1)}, u32[]{:S(2)}) %copy-start) | copy-done | bytes 16777240
  81.6 6.3 %add_convert_fusion.2 = bf16[16,2,64,256]{3,2,1,0:T(8,128)(2,1)} fusion(f32[16,2,64,256]{3,2,1,0:T(8,128)S(1)} %bitcast.123, f32[16,2,64,256]{3,2,1,0:T(8,128)} %bitcast.124, f32[16,2,64,256]{3,2,1,0:T(8,128)} %bitcast.125, f32[16,2,64,256]{3,2,1,0:T(8,128)} %bitcast.126, f32[16,2,64,256]{3,2,1,0:T(8,128)} %bitcast.127, f32[16,2,64,256]{3,2,1,0:T(8,128)} %bitcast.128, ...), kind=kLoop, calls=%fused_computation.37 | loop fusion | flops 8388608 | bytes 17826816 | tf_op jit(solution)/shard_map/convert_element_type | solution.py:234
  87.9 7.2 %all-to-all-start.1 = ((bf16[16,2,64,256]{3,2,1,0:T(8,128)(2,1)}), bf16[16,2,64,256]{3,2,1,0:T(8,128)(2,1)S(1)}, u32[]{:S(2)}, u32[]{:S(2)}) async-start(bf16[16,2,64,256]{3,2,1,0:T(8,128)(2,1)} %add_convert_fusion.2), calls=%async_computation.1 | async-start | bytes 2097152 | tf_op jit(solution)/shard_map/all_to_all | solution.py:233
  95.2 4.0 %constant_dynamic-update-slice_fusion.2 = (f32[8,32,64,256]{3,2,1,0:T(8,128)}, f32[1,32,64,256]{3,2,1,0:T(8,128)S(1)}) fusion(f32[8,32,64,256]{3,2,1,0:T(8,128)} %get-tuple-element.32, f32[8,32,64,256]{3,2,1,0:T(8,128)} %copy-done, f32[32]{0:T(128)} %get-tuple-element.80, f32[32]{0:T(128)} %get-tuple-element.79), kind=kLoop, calls=%fused_computation.119 | loop fusion | flops 1572864 | bytes 8389632
  99.2 3.3 %fusion.31 = f32[8,32,64,256]{3,2,1,0:T(8,128)} fusion(f32[8,32,64,256]{3,2,1,0:T(8,128)} %get-tuple-element.29, f32[1,32,64,256]{3,2,1,0:T(8,128)S(1)} %get-tuple-element.30, f32[32]{0:T(128)S(1)} %copy-done.24, f32[8,32,64,256]{3,2,1,0:T(8,128)} %copy-done), kind=kLoop, calls=%fused_computation.70 | loop fusion | flops 1048576 | bytes 6291584
  102.6 4.1 %constant_dynamic-update-slice_fusion.1 = (f32[8,32,64,256]{3,2,1,0:T(8,128)}, f32[1,32,64,256]{3,2,1,0:T(8,128)S(1)}) fusion(f32[8,32,64,256]{3,2,1,0:T(8,128)} %fusion.31, f32[8,32,64,256]{3,2,1,0:T(8,128)} %copy-done, f32[1,32,64,256]{3,2,1,0:T(8,128)S(1)} %get-tuple-element.30, f32[32]{0:T(128)S(1)} %copy-done.24, f32[32]{0:T(128)S(1)} %copy-done.33), kind=kLoop, calls=%fused_computation.118 | loop fusion | flops 2097152 | bytes 10486016
  106.7 5.6 %all-to-all-done.1 = bf16[16,2,64,256]{3,2,1,0:T(8,128)(2,1)S(1)} async-done(((bf16[16,2,64,256]{3,2,1,0:T(8,128)(2,1)}), bf16[16,2,64,256]{3,2,1,0:T(8,128)(2,1)S(1)}, u32[]{:S(2)}, u32[]{:S(2)}) %all-to-all-start.1) | async-done | bytes 1048608 | tf_op jit(solution)/shard_map/all_to_all | solution.py:233
  123.3 5.1 %all-to-all-start.2 = ((bf16[16,2,64,256]{3,2,1,0:T(8,128)(2,1)}), bf16[16,2,64,256]{3,2,1,0:T(8,128)(2,1)}, u32[]{:S(2)}, u32[]{:S(2)}) async-start(bf16[16,2,64,256]{3,2,1,0:T(8,128)(2,1)} %fusion.49), calls=%async_computation.2 | async-start | bytes 2097152 | tf_op jit(solution)/shard_map/all_to_all | solution.py:243
  128.4 3.2 %fusion.32 = f32[8,32,64,256]{3,2,1,0:T(8,128)} fusion(f32[8,32,64,256]{3,2,1,0:T(8,128)} %get-tuple-element.27, f32[1,32,64,256]{3,2,1,0:T(8,128)S(1)} %get-tuple-element.28, f32[32]{0:T(128)S(1)} %copy-done.19, f32[8,32,64,256]{3,2,1,0:T(8,128)} %copy-done), kind=kLoop, calls=%fused_computation.71 | loop fusion | flops 1048576 | bytes 6291584
  131.6 4.0 %constant_dynamic-update-slice_fusion = (f32[8,32,64,256]{3,2,1,0:T(8,128)}, f32[1,32,64,256]{3,2,1,0:T(8,128)S(1)}) fusion(f32[8,32,64,256]{3,2,1,0:T(8,128)} %fusion.32, f32[8,32,64,256]{3,2,1,0:T(8,128)} %copy-done, f32[1,32,64,256]{3,2,1,0:T(8,128)S(1)} %get-tuple-element.28, f32[32]{0:T(128)S(1)} %copy-done.19, f32[32]{0:T(128)S(1)} %copy-done.28), kind=kLoop, calls=%fused_computation.117 | loop fusion | flops 2097152 | bytes 10486016
  135.6 3.2 %add_dynamic-update-slice_fusion = f32[8,32,64,256]{3,2,1,0:T(8,128)} fusion(f32[8,32,64,256]{3,2,1,0:T(8,128)} %get-tuple-element.25, f32[1,32,64,256]{3,2,1,0:T(8,128)S(1)} %get-tuple-element.26, f32[32]{0:T(128)S(1)} %copy-done.27, f32[8,32,64,256]{3,2,1,0:T(8,128)} %copy-done), kind=kLoop, calls=%fused_computation.38 | loop fusion | flops 1048576 | bytes 6291584 | tf_op jit(solution)/shard_map/stack | solution.py:248
  138.8 6.9 %all-to-all-done.2 = bf16[16,2,64,256]{3,2,1,0:T(8,128)(2,1)} async-done(((bf16[16,2,64,256]{3,2,1,0:T(8,128)(2,1)}), bf16[16,2,64,256]{3,2,1,0:T(8,128)(2,1)}, u32[]{:S(2)}, u32[]{:S(2)}) %all-to-all-start.2) | async-done | bytes 1048608 | tf_op jit(solution)/shard_map/all_to_all | solution.py:243
  145.8 1.5 bitcast_convert_fusion
  147.3 11.9 %fusion.7 = f32[8,128,32,64]{1,3,2,0:T(8,128)} fusion(bf16[8,128,256,1]{2,1,3,0:T(8,128)(2,1)} %bitcast.133, f32[8,32,64,256]{3,2,1,0:T(8,128)} %add_dynamic-update-slice_fusion, f32[32,64,256]{2,1,0:T(8,128)S(1)} %bitcast_convert_fusion, f32[8,32]{1,0:T(8,128)S(1)} %copy-done.12), kind=kOutput, calls=%fused_computation.13 | convolution fusion | flops 1086324736 | bytes 27788288 | tf_op jit(solution)/shard_map/ctn,chpn->cthp/dot_general | solution.py:251
  159.3 12.6 %fusion.2 = f32[8,128,32,64]{1,3,2,0:T(8,128)} fusion(bf16[8,128,32,64]{1,3,2,0:T(8,128)(2,1)S(1)} %copy-done.2, f32[8,128,32,64]{1,3,2,0:T(8,128)} %fusion.7, f32[32]{0:T(128)S(1)} %copy-done.37, f32[8,128,32]{1,2,0:T(8,128)S(1)} %copy-done.8, f32[8,32,128]{2,1,0:T(8,128)S(1)} %copy-done.9, f32[8,32,128]{2,1,0:T(8,128)S(1)} %copy-done.7, ...), kind=kOutput, calls=%fused_computation.8 | convolution fusion | flops 572522496 | bytes 21905536 | tf_op jit(solution)/shard_map/chts,cshp->cthp/dot_general | solution.py:217
  171.9 16.2 %copy.37 = f32[8,128,32,64]{3,2,1,0:T(8,128)} copy(f32[8,128,32,64]{1,3,2,0:T(8,128)} %fusion.2) | data formatting | bytes 16777216 | tf_op jit(solution)/shard_map/reshape | solution.py:256
  188.1 14.9 %reshape.182 = f32[1024,2048]{1,0:T(8,128)} reshape(f32[8,128,32,64]{3,2,1,0:T(8,128)} %copy.37) | data formatting | bytes 16777216 | tf_op jit(solution)/shard_map/reshape | solution.py:256
  203.0 6.2 %multiply_reduce_fusion = f32[1024]{0:T(1024)S(1)} fusion(f32[1024,2048]{1,0:T(8,128)} %reshape.182, bf16[1024,2048]{1,0:T(8,128)(2,1)} %param.15), kind=kLoop, calls=%fused_computation.24 | loop fusion | flops 16776192 | bytes 12587008 | tf_op jit(solution)/shard_map/reduce_sum | solution.py:257
  211.2 5.3 %multiply_convert_fusion.2.normed_ref = bf16[1024,2048]{1,0:T(8,128)(2,1)} fusion(f32[2048]{0:T(1024)S(1)} %copy-done.16, f32[1024]{0:T(1024)S(1)} %add_rsqrt_fusion, f32[1024,2048]{1,0:T(8,128)S(1)} %copy-done.1, bf16[1024,2048]{1,0:T(8,128)(2,1)S(1)} %copy-done.3), kind=kLoop, calls=%fused_computation.23 | loop fusion | flops 18874368 | bytes 16789504 | tf_op jit(solution)/shard_map/convert_element_type | solution.py:258
  216.5 86.4 %project.1 = bf16[128,4096]{1,0:T(8,128)(2,1)} custom-call(bf16[1024,2048]{1,0:T(8,128)(2,1)} %multiply_convert_fusion.2.normed_ref, bf16[2048,4096]{1,0:T(8,128)(2,1)} %weight_ref.1), custom_call_target="tpu_custom_call" | custom-call | tf_op jit(solution)/shard_map/project/pallas_call | solution.py:132
  302.9 2.3 copy.70
  (129 shorter events, 29.0 us)
Async XLA Ops:
  0.0 25.9 %copy-start.18 = (f32[2,4,256]{2,1,0:T(4,128)S(1)}, f32[2,4,256]{2,1,0:T(4,128)}, u32[]{:S(2)}) copy-start(f32[2,4,256]{2,1,0:T(4,128)} %param.18) | copy-start | bytes 24580
  0.0 25.9 %copy-start.36 = (f32[2,256]{1,0:T(2,128)S(1)}, f32[2,256]{1,0:T(2,128)}, u32[]{:S(2)}) copy-start(f32[2,256]{1,0:T(2,128)} %param.20) | copy-start | bytes 6148
  0.0 26.0 %copy-start.10 = (f32[4,2048]{1,0:T(4,128)S(1)}, f32[4,2048]{1,0:T(4,128)}, u32[]{:S(2)}) copy-start(f32[4,2048]{1,0:T(4,128)} %param.17) | copy-start | bytes 98308
  0.8 30.4 %collective-permute-start.1 = (bf16[2,3,256]{2,1,0:T(4,128)(2,1)S(1)}, bf16[2,3,256]{2,1,0:T(4,128)(2,1)S(1)}, u32[]{:S(2)}, u32[]{:S(2)}) collective-permute-start(bf16[2,3,256]{2,1,0:T(4,128)(2,1)S(1)} %slice.282), channel_id=1, source_target_pairs={{0,8},{8,16},{16,24},{24,32},{32,40},{40,48},{48,56},{56,64},{64,7... | collective-permute-start | bytes 9224 | tf_op jit(solution)/shard_map/ppermute | solution.py:22
  7.6 26.4 %collective-permute-start = (bf16[3,2048]{1,0:T(4,128)(2,1)S(1)}, bf16[3,2048]{1,0:T(4,128)(2,1)S(1)}, u32[]{:S(2)}, u32[]{:S(2)}) collective-permute-start(bf16[3,2048]{1,0:T(4,128)(2,1)S(1)} %slice.272), channel_id=1, source_target_pairs={{0,8},{8,16},{16,24},{24,32},{32,40},{40,48},{48,56},{56,64},{64,7... | collective-permute-start | bytes 36872 | tf_op jit(solution)/shard_map/ppermute | solution.py:22
  13.5 17.9 %copy-start.6 = (f32[8,32,128]{2,1,0:T(8,128)}, f32[8,32,128]{2,1,0:T(8,128)S(1)}, u32[]{:S(2)}) copy-start(f32[8,32,128]{2,1,0:T(8,128)S(1)} %reduce_window_sum.22) | copy-start | bytes 393220
  14.4 16.1 %all-to-all-start = ((f32[16,1,2]{2,1,0:T(1,128)}), f32[16,1,2]{2,1,0:T(1,128)S(1)}, u32[]{:S(2)}, u32[]{:S(2)}) async-start(f32[16,1,2]{2,1,0:T(1,128)} %bitcast.36), calls=%async_computation | async-start | bytes 16384 | tf_op jit(solution)/shard_map/all_to_all | solution.py:236
  71.5 10.1 %copy-start = (f32[8,32,64,256]{3,2,1,0:T(8,128)}, f32[8,32,64,256]{3,2,1,0:T(8,128)S(1)}, u32[]{:S(2)}) copy-start(f32[8,32,64,256]{3,2,1,0:T(8,128)S(1)} %fusion.20) | copy-start | bytes 50331652
  87.9 24.4 %all-to-all-start.1 = ((bf16[16,2,64,256]{3,2,1,0:T(8,128)(2,1)}), bf16[16,2,64,256]{3,2,1,0:T(8,128)(2,1)S(1)}, u32[]{:S(2)}, u32[]{:S(2)}) async-start(bf16[16,2,64,256]{3,2,1,0:T(8,128)(2,1)} %add_convert_fusion.2), calls=%async_computation.1 | async-start | bytes 2097152 | tf_op jit(solution)/shard_map/all_to_all | solution.py:233
  102.5 10.6 %copy-start.14 = (f32[2]{0:T(128)S(1)}, f32[2]{0:T(128)}, u32[]{:S(2)}) copy-start(f32[2]{0:T(128)} %get-tuple-element.62) | copy-start | bytes 28
  102.5 11.3 %copy-start.17 = (f32[2]{0:T(128)S(1)}, f32[2]{0:T(128)}, u32[]{:S(2)}) copy-start(f32[2]{0:T(128)} %get-tuple-element.61) | copy-start | bytes 28
  102.5 12.1 %copy-start.26 = (f32[2]{0:T(128)S(1)}, f32[2]{0:T(128)}, u32[]{:S(2)}) copy-start(f32[2]{0:T(128)} %get-tuple-element.60) | copy-start | bytes 28
  102.5 12.8 %copy-start.35 = (f32[2]{0:T(128)S(1)}, f32[2]{0:T(128)}, u32[]{:S(2)}) copy-start(f32[2]{0:T(128)} %get-tuple-element.59) | copy-start | bytes 28
  102.5 13.6 %copy-start.25 = (f32[2]{0:T(128)S(1)}, f32[2]{0:T(128)}, u32[]{:S(2)}) copy-start(f32[2]{0:T(128)} %get-tuple-element.58) | copy-start | bytes 28
  102.5 14.3 %copy-start.34 = (f32[2]{0:T(128)S(1)}, f32[2]{0:T(128)}, u32[]{:S(2)}) copy-start(f32[2]{0:T(128)} %get-tuple-element.57) | copy-start | bytes 28
  102.5 15.0 %copy-start.23 = (f32[2]{0:T(128)S(1)}, f32[2]{0:T(128)}, u32[]{:S(2)}) copy-start(f32[2]{0:T(128)} %get-tuple-element.56) | copy-start | bytes 28
  102.5 15.7 %copy-start.32 = (f32[2]{0:T(128)S(1)}, f32[2]{0:T(128)}, u32[]{:S(2)}) copy-start(f32[2]{0:T(128)} %get-tuple-element.55) | copy-start | bytes 28
  102.5 16.4 %copy-start.22 = (f32[2]{0:T(128)S(1)}, f32[2]{0:T(128)}, u32[]{:S(2)}) copy-start(f32[2]{0:T(128)} %get-tuple-element.54) | copy-start | bytes 28
  102.5 17.1 %copy-start.31 = (f32[2]{0:T(128)S(1)}, f32[2]{0:T(128)}, u32[]{:S(2)}) copy-start(f32[2]{0:T(128)} %get-tuple-element.53) | copy-start | bytes 28
  102.5 17.8 %copy-start.21 = (f32[2]{0:T(128)S(1)}, f32[2]{0:T(128)}, u32[]{:S(2)}) copy-start(f32[2]{0:T(128)} %get-tuple-element.52) | copy-start | bytes 28
  102.6 18.5 %copy-start.30 = (f32[2]{0:T(128)S(1)}, f32[2]{0:T(128)}, u32[]{:S(2)}) copy-start(f32[2]{0:T(128)} %get-tuple-element.51) | copy-start | bytes 28
  106.7 15.1 %copy-start.20 = (f32[2]{0:T(128)S(1)}, f32[2]{0:T(128)}, u32[]{:S(2)}) copy-start(f32[2]{0:T(128)} %get-tuple-element.50) | copy-start | bytes 28
  106.7 15.8 %copy-start.29 = (f32[2]{0:T(128)S(1)}, f32[2]{0:T(128)}, u32[]{:S(2)}) copy-start(f32[2]{0:T(128)} %get-tuple-element.49) | copy-start | bytes 28
  106.7 21.7 %copy-start.19 = (f32[32]{0:T(128)S(1)}, f32[32]{0:T(128)}, u32[]{:S(2)}) copy-start(f32[32]{0:T(128)} %get-tuple-element.76) | copy-start | bytes 388
  123.3 22.5 %all-to-all-start.2 = ((bf16[16,2,64,256]{3,2,1,0:T(8,128)(2,1)}), bf16[16,2,64,256]{3,2,1,0:T(8,128)(2,1)}, u32[]{:S(2)}, u32[]{:S(2)}) async-start(bf16[16,2,64,256]{3,2,1,0:T(8,128)(2,1)} %fusion.49), calls=%async_computation.2 | async-start | bytes 2097152 | tf_op jit(solution)/shard_map/all_to_all | solution.py:243
  135.6 11.7 %copy-start.12 = (f32[8,32]{1,0:T(8,128)S(1)}, f32[8,32]{1,0:T(8,128)}, u32[]{:S(2)}) copy-start(f32[8,32]{1,0:T(8,128)} %get-tuple-element.72) | copy-start | bytes 3076
  147.3 12.0 %copy-start.2 = (bf16[8,128,32,64]{1,3,2,0:T(8,128)(2,1)S(1)}, bf16[8,128,32,64]{1,3,2,0:T(8,128)(2,1)}, u32[]{:S(2)}) copy-start(bf16[8,128,32,64]{1,3,2,0:T(8,128)(2,1)} %copy.29) | copy-start | bytes 12582916
  147.3 12.0 %copy-start.7 = (f32[8,32,128]{2,1,0:T(8,128)S(1)}, f32[8,32,128]{2,1,0:T(8,128)}, u32[]{:S(2)}) copy-start(f32[8,32,128]{2,1,0:T(8,128)} %copy-done.6) | copy-start | bytes 393220
  147.3 12.0 %copy-start.8 = (f32[8,128,32]{1,2,0:T(8,128)S(1)}, f32[8,128,32]{1,2,0:T(8,128)}, u32[]{:S(2)}) copy-start(f32[8,128,32]{1,2,0:T(8,128)} %exponential_bitcast_fusion) | copy-start | bytes 393220
  147.3 12.0 %copy-start.9 = (f32[8,32,128]{2,1,0:T(8,128)S(1)}, f32[8,32,128]{2,1,0:T(8,128)}, u32[]{:S(2)}) copy-start(f32[8,32,128]{2,1,0:T(8,128)} %copy.28) | copy-start | bytes 393220
  147.3 12.0 %copy-start.13 = (pred[128,128]{1,0:T(8,128)(4,1)S(1)}, pred[128,128]{1,0:T(8,128)(4,1)}, u32[]{:S(2)}) copy-start(pred[128,128]{1,0:T(8,128)(4,1)} %iota_compare_fusion) | copy-start | bytes 49156
  147.3 12.0 %copy-start.37 = (f32[32]{0:T(128)S(1)}, f32[32]{0:T(128)}, u32[]{:S(2)}) copy-start(f32[32]{0:T(128)} %param.23) | copy-start | bytes 388
  (11 other events, 58.7 us)

commit v2 on v1

v2 whole, which is shorter than its diff:
```python
import functools

import jax
import jax.numpy as jnp
from jax import lax
from jax.experimental import pallas as pl
from jax.experimental.pallas import tpu as pltpu
from jax.sharding import PartitionSpec as P

H = 256
P_SIZE = 64
N = 256
G = 8
KW = 4
BLOCK = 128
MESH = pl.DeviceIdType.MESH


LOG2E = 1.4426950408889634
FAR = -1e30
F32 = jnp.float32
BF16 = jnp.bfloat16


def dot(left, right, **options):
    return jnp.dot(left, right, preferred_element_type=F32, **options)


def silu(v):
    return 0.5 * v * (1.0 + jnp.tanh(0.5 * v))


def split(v):
    high = v.astype(BF16)
    left = v - high.astype(F32)
    middle = left.astype(BF16)
    low = (left - middle.astype(F32)).astype(BF16)
    return jnp.concatenate([high, middle, low], axis=1)


def spreading(heads):
    shape = (3 * heads, heads * P_SIZE)
    row = lax.broadcasted_iota(jnp.int32, shape, 0)
    lane = lax.broadcasted_iota(jnp.int32, shape, 1)
    hit = lax.rem(row, heads) == lax.shift_right_logical(lane, 6)
    return jnp.where(hit, 1.0, 0.0).astype(BF16)


STEP = 256
SCAN_AFTER = 3


def front_kernel(devices, x_ref, bc_ref, dt_ref, xw_ref, bw_ref, xb_ref, bb_ref, off_ref, dlog_ref,
                 skip_ref, y_hbm, c_ref, lead_ref, incoming_ref,
                 hx, hbc, xf, xc, bt, cumcol, rowt, fend, ec, spread, rowexp, total, carry, before,
                 stage, ends, got, pref, inc,
                 hx_sems, hbc_sems, esend, erecv, psend, precv, ysem):
    me = lax.axis_index("seq")
    tokens, width = x_ref.shape
    blocks = tokens // BLOCK
    heads = dt_ref.shape[1]
    steps = width // STEP
    barrier = pltpu.get_barrier_semaphore()

    @pl.loop(1, devices)
    def _(k):
        pl.semaphore_signal(barrier, inc=1, device_id={"seq": lax.rem(me + k, devices)},
                            device_id_type=MESH)

    pl.semaphore_wait(barrier, devices - 1)

    after = {"seq": lax.rem(me + 1, devices)}
    halo_x = pltpu.make_async_remote_copy(
        src_ref=x_ref.at[tokens - 16 :, :], dst_ref=hx, send_sem=hx_sems.at[0],
        recv_sem=hx_sems.at[1], device_id=after, device_id_type=MESH)
    halo_bc = pltpu.make_async_remote_copy(
        src_ref=bc_ref.at[:, tokens - 16 :, :], dst_ref=hbc, send_sem=hbc_sems.at[0],
        recv_sem=hbc_sems.at[1], device_id=after, device_id_type=MESH)
    halo_bc.start()
    halo_x.start()

    spread[...] = spreading(heads)
    steps_dt = dt_ref[...].astype(F32) + off_ref[...]
    steps_dt = jnp.maximum(steps_dt, 0.0) + jnp.log1p(jnp.exp(-jnp.abs(steps_dt)))
    log_decay = steps_dt * (-LOG2E * jnp.exp(dlog_ref[...]))
    at = lax.broadcasted_iota(jnp.int32, (BLOCK, BLOCK), 0)
    to = lax.broadcasted_iota(jnp.int32, (BLOCK, BLOCK), 1)
    causal = at >= to
    lower = jnp.where(causal, 1.0, 0.0).astype(F32)
    lead = jnp.zeros((1, heads), F32)
    rows_of = []
    for b in range(blocks):
        here = slice(b * BLOCK, (b + 1) * BLOCK)
        dt_here = steps_dt[here]
        cumul = dot(lower, log_decay[here], precision=lax.Precision.HIGHEST)
        end = cumul[BLOCK - 1 :, :]
        cumcol[here, :] = cumul
        rowt[b] = (cumul - LOG2E * jnp.log(dt_here)).T
        fend[here, :] = split(jnp.exp2(end - cumul) * dt_here)
        ec[here, :] = split(jnp.exp2(cumul))
        lead_ref[here, :] = split(jnp.exp2(cumul + lead))
        rows_of.append(jnp.exp2(end))
        lead = lead + end
    rows_of += [jnp.exp2(lead), skip_ref[...]]
    rows_of += [jnp.zeros((1, heads), F32)] * (16 - len(rows_of))
    rowexp[...] = dot(split(jnp.concatenate(rows_of, axis=0)), spread[...])
    whole = rowexp[blocks : blocks + 1, :]
    high = whole.astype(BF16).astype(F32)
    middle = (whole - high).astype(BF16).astype(F32)
    low = whole - high - middle
    row = lax.broadcasted_iota(jnp.int32, (16, width), 0)
    total[...] = jnp.where(
        row == 0, high, jnp.where(row == 1, middle, jnp.where(row == 2, low, 0.0))
    ).astype(BF16)

    first = jnp.where(me > 0, 1.0, 0.0).astype(F32)

    def conv(rows, weights, bias):
        acc = bias + weights[0] * xf[rows + 5 : rows + 5 + BLOCK, :]
        for k in range(1, KW):
            acc = acc + weights[k] * xf[rows + 5 + k : rows + 5 + k + BLOCK, :]
        return silu(acc).astype(BF16)

    halo_bc.wait_recv()
    for i in (0, 1):
        xf[0:8, :] = hbc[i, 8:16, :].astype(F32) * first
        xf[8:, :] = bc_ref[i].astype(F32)
        for b in range(blocks):
            done = conv(b * BLOCK, [bw_ref[i, k : k + 1, :] for k in range(KW)], bb_ref[i : i + 1, :])
            if i == 0:
                bt[b] = done.astype(F32).T.astype(BF16)
            else:
                c_ref[b * BLOCK : (b + 1) * BLOCK, :] = done

    def send_end(owner):
        return pltpu.make_async_remote_copy(
            src_ref=ends.at[owner], dst_ref=got.at[me], send_sem=esend.at[owner],
            recv_sem=erecv.at[me], device_id={"seq": owner}, device_id_type=MESH)

    def send_prefix(target):
        return pltpu.make_async_remote_copy(
            src_ref=pref.at[target], dst_ref=inc.at[me], send_sem=psend.at[target],
            recv_sem=precv.at[me], device_id={"seq": target}, device_id_type=MESH)

    halo_x.wait_recv()

    @pl.loop(0, steps)
    def _(k):
        step = lax.rem(me // 2 + 1 + k, steps)
        lane0 = pl.multiple_of(step * STEP, STEP)
        lanes = pl.ds(lane0, STEP)
        xf[0:8, :] = hx[8:16, lanes].astype(F32) * first
        xf[8:, :] = x_ref[:, lanes].astype(F32)
        weights = [xw_ref[i : i + 1, lanes] for i in range(KW)]
        bias = xb_ref[0:1, lanes]
        carry[...] = jnp.zeros_like(carry)
        for b in range(blocks):
            here = slice(b * BLOCK, (b + 1) * BLOCK)
            done = conv(b * BLOCK, weights, bias)
            xc[here, lanes] = done
            weighted = (done.astype(F32) * dot(fend[here, :], spread[:, lanes])).astype(BF16)
            run = carry[...]
            before[b, :, lanes] = run.astype(BF16)
            carry[...] = rowexp[b : b + 1, lanes] * run + dot(bt[b], weighted)
        for half in (0, 1):
            owner = step * 2 + half
            ends[owner, 0:N, :] = carry[:, half * 128 : (half + 1) * 128].astype(BF16)
            ends[owner, N:, :] = total[:, pl.ds(pl.multiple_of(lane0 + half * 128, 128), 128)]

            @pl.when(owner != me)
            def _():
                send_end(owner).start()

    def store_y(b):
        return pltpu.make_async_copy(
            stage.at[b], y_hbm.at[pl.ds(pl.multiple_of(b * BLOCK, BLOCK), BLOCK), :], ysem.at[b])

    left_half = lax.broadcasted_iota(jnp.int32, (BLOCK, 128), 1) < P_SIZE

    def block_step(b):
        here = pl.ds(pl.multiple_of(b * BLOCK, BLOCK), BLOCK)
        c_here = c_ref[here, :]
        inner = dot(c_here, bt[b])
        for quad in range(steps):
            lanes = slice(quad * STEP, (quad + 1) * STEP)
            sides = []
            for pair in (0, 1):
                scores = []
                for odd in (0, 1):
                    h = quad * 4 + pair * 2 + odd
                    gap = cumcol[here, h : h + 1] - rowt[b, h : h + 1, :]
                    scores.append((inner * jnp.exp2(jnp.where(causal, gap, FAR))).astype(BF16))
                x_here = xc[here, quad * STEP + pair * 128 : quad * STEP + (pair + 1) * 128]
                zero = jnp.zeros_like(x_here)
                both = jnp.concatenate(
                    [jnp.where(left_half, x_here, zero), jnp.where(left_half, zero, x_here)], axis=0)
                sides.append(dot(jnp.concatenate(scores, axis=1), both))
            y = jnp.concatenate(sides, axis=1)
            y = y + dot(ec[here, :], spread[:, lanes]) * dot(c_here, before[b, :, lanes])
            y = y + rowexp[blocks + 1 : blocks + 2, lanes] * xc[here, lanes].astype(F32)
            stage[b, :, lanes] = y
        store_y(b).start()

    pl.loop(0, SCAN_AFTER)(block_step)

    got[me] = ends[me]
    carry[:, :128] = jnp.zeros((N, 128), F32)

    @pl.loop(0, devices)
    def _(i):
        run = carry[:, :128]

        @pl.when(i != me)
        def _():
            pref[i] = run.astype(BF16)
            send_prefix(i).start()
            pltpu.make_async_remote_copy(
                src_ref=ends.at[i], dst_ref=got.at[i], send_sem=esend.at[i], recv_sem=erecv.at[i],
                device_id={"seq": i}, device_id_type=MESH).wait_recv()

        @pl.when(i == me)
        def _():
            inc[me] = run.astype(BF16)

        factor = jnp.sum(got[i, N:, :].astype(F32), axis=0, keepdims=True)
        carry[:, :128] = factor * run + got[i, :N, :].astype(F32)

    pl.loop(SCAN_AFTER, blocks)(block_step)

    @pl.loop(1, devices)
    def _(k):
        other = lax.rem(me + k, devices)
        pltpu.make_async_remote_copy(
            src_ref=pref.at[other], dst_ref=inc.at[other], send_sem=psend.at[other],
            recv_sem=precv.at[other], device_id={"seq": other}, device_id_type=MESH).wait_recv()

    for j in range(devices):
        incoming_ref[:, j * 128 : (j + 1) * 128] = inc[j]

    @pl.loop(1, devices)
    def _(k):
        other = lax.rem(me + k, devices)
        send_end(other).wait_send()
        send_prefix(other).wait_send()

    halo_bc.wait_send()
    halo_x.wait_send()

    @pl.loop(0, blocks)
    def _(b):
        store_y(b).wait()


def front(devices, x, bc, dt, xw, bw, xb, bb, offset, decay_log, skip):
    tokens, width = x.shape
    heads = dt.shape[1]
    blocks = tokens // BLOCK
    dma = pltpu.SemaphoreType.DMA
    vmem = pl.BlockSpec(memory_space=pltpu.VMEM)
    return pl.pallas_call(
        functools.partial(front_kernel, devices),
        out_shape=(
            jax.ShapeDtypeStruct((tokens, width), F32),
            jax.ShapeDtypeStruct((tokens, N), BF16),
            jax.ShapeDtypeStruct((tokens, 3 * heads), BF16),
            jax.ShapeDtypeStruct((N, width), BF16),
        ),
        in_specs=[vmem] * 10,
        out_specs=(pl.BlockSpec(memory_space=pl.ANY), vmem, vmem, vmem),
        scratch_shapes=[
            pltpu.VMEM((16, width), BF16),
            pltpu.VMEM((2, 16, N), BF16),
            pltpu.VMEM((8 + tokens, STEP), F32),
            pltpu.VMEM((tokens, width), BF16),
            pltpu.VMEM((blocks, N, BLOCK), BF16),
            pltpu.VMEM((tokens, heads), F32),
            pltpu.VMEM((blocks, heads, BLOCK), F32),
            pltpu.VMEM((tokens, 3 * heads), BF16),
            pltpu.VMEM((tokens, 3 * heads), BF16),
            pltpu.VMEM((3 * heads, width), BF16),
            pltpu.VMEM((16, width), F32),
            pltpu.VMEM((16, width), BF16),
            pltpu.VMEM((N, STEP), F32),
            pltpu.VMEM((blocks, N, width), BF16),
            pltpu.VMEM((blocks, BLOCK, width), F32),
            pltpu.VMEM((devices, N + 16, 128), BF16),
            pltpu.VMEM((devices, N + 16, 128), BF16),
            pltpu.VMEM((devices, N, 128), BF16),
            pltpu.VMEM((devices, N, 128), BF16),
            dma((2,)),
            dma((2,)),
            dma((devices,)),
            dma((devices,)),
            dma((devices,)),
            dma((devices,)),
            dma((blocks,)),
        ],
        compiler_params=pltpu.CompilerParams(
            collective_id=2, has_side_effects=True, vmem_limit_bytes=60 * 1024 * 1024
        ),
        name="front",
    )(x, bc, dt, xw, bw, xb, bb, offset, decay_log, skip)


CHUNKS = 4
TILE = 256


def project_kernel(rows, y_ref, c_ref, lead_ref, incoming_ref, z_ref, gain_ref, weight_ref, out_ref,
                   ybuf, zbuf, spread, gated, normed, w, sent, got, kept, xsent, xgot,
                   ysem, zsem, wsem, send_sem, recv_sem, xsend_sem, xrecv_sem):
    head = lax.axis_index("head")
    y = head // 2
    x = lax.rem(head, 2)
    wide = out_ref.shape[1] // CHUNKS
    up = {"head": lax.rem(y + 1, 4) * 2 + x}
    down = {"head": lax.rem(y + 3, 4) * 2 + x}
    across = {"head": y * 2 + 1 - x}
    blocks = y_ref.shape[0] // rows
    width = y_ref.shape[1]

    def needed(s):
        return lax.rem(y + 3 - s, 4) * 2 + 1 - x, lax.rem(y + 1 + s, 4) * 2 + x

    def rows_in(s):
        copies = []
        for block in needed(s):
            here = pl.ds(pl.multiple_of(block * rows, rows), rows)
            copies.append(pltpu.make_async_copy(y_ref.at[here, :], ybuf.at[block], ysem.at[block]))
            copies.append(pltpu.make_async_copy(z_ref.at[here, :], zbuf.at[block], zsem.at[block]))
        return copies

    for copy in rows_in(0):
        copy.start()
    loads = []
    for c in range(CHUNKS):
        load = pltpu.make_async_copy(
            weight_ref.at[:, c * wide : (c + 1) * wide], w.at[c], wsem.at[c]
        )
        load.start()
        loads.append(load)
        if c == 0:
            for s in range(1, 4):
                for copy in rows_in(s):
                    copy.start()
    spread[...] = spreading(lead_ref.shape[1] // 3)

    def normalise(block):
        here = pl.ds(pl.multiple_of(block * rows, rows), rows)
        c_here = c_ref[here, :]
        lead_here = lead_ref[here, :]
        square = jnp.zeros((rows, 128), F32)
        for t in range(width // TILE):
            lanes = slice(t * TILE, (t + 1) * TILE)
            y_here = ybuf[block, :, lanes] + dot(lead_here, spread[:, lanes]) * dot(
                c_here, incoming_ref[:, lanes]
            )
            value = y_here * silu(zbuf[block, :, lanes].astype(F32))
            gated[:, lanes] = value
            for part in range(TILE // 128):
                piece = value[:, part * 128 : (part + 1) * 128]
                square = square + piece * piece
        scale = lax.rsqrt(jnp.sum(square, axis=1, keepdims=True) / width + 1e-05)
        for t in range(width // TILE):
            lanes = slice(t * TILE, (t + 1) * TILE)
            normed[here, lanes] = (gated[:, lanes] * scale * gain_ref[:, lanes]).astype(BF16)

    barrier = pltpu.get_barrier_semaphore()
    for to in (up, down, across):
        pl.semaphore_signal(barrier, inc=1, device_id=to, device_id_type=MESH)
    pl.semaphore_wait(barrier, 3)

    def ring(c, s, role):
        return pltpu.make_async_remote_copy(
            src_ref=sent.at[c, s, role],
            dst_ref=got.at[c, s, role],
            send_sem=send_sem.at[c, s, role],
            recv_sem=recv_sem.at[c, s, role],
            device_id=up if role == 0 else down,
            device_id_type=MESH,
        )

    def cross(c):
        return pltpu.make_async_remote_copy(
            src_ref=xsent.at[c],
            dst_ref=xgot.at[c],
            send_sem=xsend_sem.at[c],
            recv_sem=xrecv_sem.at[c],
            device_id=across,
            device_id_type=MESH,
        )

    def event(c, s):
        if s == 0:
            loads[c].wait()
        if c == 0:
            for copy in rows_in(s):
                copy.wait()

            @pl.loop(0, 2)
            def _(role):
                block0, block1 = needed(s)
                normalise(jnp.where(role == 0, block0, block1))

        if s > 0:
            for role in (0, 1):
                ring(c, s - 1, role).wait_recv()
        block0, block1 = needed(s)
        row0 = pl.multiple_of(block0 * rows, rows)
        row1 = pl.multiple_of(block1 * rows, rows)

        @pl.loop(0, wide // TILE)
        def _(t):
            cols = pl.ds(pl.multiple_of(t * TILE, TILE), TILE)
            left = jnp.concatenate(
                [normed[pl.ds(row0, rows), :], normed[pl.ds(row1, rows), :]], axis=0
            )
            part = jnp.dot(left, w[c, :, cols], preferred_element_type=jnp.float32)
            part0, part1 = part[:rows], part[rows:]
            if s > 0:
                part0 = part0 + got[c, s - 1, 0, :, cols].astype(jnp.float32)
                part1 = part1 + got[c, s - 1, 1, :, cols].astype(jnp.float32)
            if s < 3:
                sent[c, s, 0, :, cols] = part0.astype(jnp.bfloat16)
                sent[c, s, 1, :, cols] = part1.astype(jnp.bfloat16)
            else:
                xsent[c, :, cols] = part0.astype(jnp.bfloat16)
                kept[c, :, cols] = part1

        if s < 3:
            ring(c, s, 0).start()
            ring(c, s, 1).start()
        else:
            cross(c).start()

    def finish(c):
        cross(c).wait_recv()
        out_ref[:, c * wide : (c + 1) * wide] = (
            kept[c] + xgot[c].astype(jnp.float32)
        ).astype(jnp.bfloat16)

    for c, s in ((0, 0), (1, 0), (0, 1), (1, 1), (0, 2), (1, 2), (2, 0), (0, 3), (3, 0), (1, 3),
                 (2, 1), (3, 1), (2, 2), (3, 2), (2, 3), (3, 3)):
        event(c, s)
        if s == 3 and c >= 2:
            finish(c - 2)
    finish(2)
    finish(3)
    for c in range(CHUNKS):
        cross(c).wait_send()
        for s in range(3):
            for role in (0, 1):
                ring(c, s, role).wait_send()


def project(y, c_conv, lead, incoming, z, gain, weight):
    tokens, depth = y.shape
    width = weight.shape[1]
    rows = tokens // 8
    wide = width // CHUNKS
    dma = pltpu.SemaphoreType.DMA
    vmem = pl.BlockSpec(memory_space=pltpu.VMEM)
    far = pl.BlockSpec(memory_space=pl.ANY)
    return pl.pallas_call(
        functools.partial(project_kernel, rows),
        out_shape=jax.ShapeDtypeStruct((rows, width), BF16),
        in_specs=[far, vmem, vmem, vmem, far, vmem, far],
        out_specs=vmem,
        scratch_shapes=[
            pltpu.VMEM((8, rows, depth), F32),
            pltpu.VMEM((8, rows, depth), BF16),
            pltpu.VMEM((lead.shape[1], depth), BF16),
            pltpu.VMEM((rows, depth), F32),
            pltpu.VMEM((tokens, depth), BF16),
            pltpu.VMEM((CHUNKS, depth, wide), BF16),
            pltpu.VMEM((CHUNKS, 3, 2, rows, wide), BF16),
            pltpu.VMEM((CHUNKS, 3, 2, rows, wide), BF16),
            pltpu.VMEM((CHUNKS, rows, wide), F32),
            pltpu.VMEM((CHUNKS, rows, wide), BF16),
            pltpu.VMEM((CHUNKS, rows, wide), BF16),
            dma((8,)),
            dma((8,)),
            dma((CHUNKS,)),
            dma((CHUNKS, 3, 2)),
            dma((CHUNKS, 3, 2)),
            dma((CHUNKS,)),
            dma((CHUNKS,)),
        ],
        compiler_params=pltpu.CompilerParams(
            collective_id=1, has_side_effects=True, vmem_limit_bytes=63 * 1024 * 1024
        ),
        name="project",
    )(y, c_conv, lead, incoming, z, gain, weight)


def per_device(
    x_values,
    bc_values,
    z_values,
    dt_values,
    xconv_weight,
    bconv_weight,
    xconv_bias,
    bconv_bias,
    dt_offset,
    decay_log,
    skip_gain,
    norm_gain,
    out_weight,
):
    y, c_conv, lead, incoming = front(
        lax.axis_size("seq"),
        x_values,
        bc_values,
        dt_values,
        xconv_weight,
        bconv_weight,
        xconv_bias[None, :],
        bconv_bias,
        dt_offset[None, :],
        decay_log[None, :],
        skip_gain[None, :],
    )
    return project(y, c_conv, lead, incoming, z_values, norm_gain[None, :], out_weight)


def solution(mesh):
    return jax.shard_map(
        per_device,
        mesh=mesh,
        in_specs=(
            P("seq", "head"),
            P(None, "seq", "head"),
            P("seq", "head"),
            P("seq", "head"),
            P(None, "head"),
            P(None, None, "head"),
            P("head"),
            P(None, "head"),
            P("head"),
            P("head"),
            P("head"),
            P("head"),
            P("head", None),
        ),
        out_specs=P(("seq", "head"), None),
        check_vma=False,
    )
```

time: 308 us -> 144 us (0.47)
  other arithmetic: 74.8 us -> 0 us
  local copies, waits for them, and re-layouts: 73.9 us -> 3.97 us
  Pallas kernels: 86.4 us -> 138 us
  matrix products: 30.2 us -> 0 us
  starting transfers between devices: 27 us -> 0 us
  waiting for transfers between devices: 12.6 us -> 0 us
    reshape x5 -> x0, local copies, waits for them, and re-layouts: 55.4 us -> none  [the longest x2 31.1 us: per_device(): total.reshape(rows_here, width) * jax.nn.silu(z_values.astype(jnp.float32))]
    pallas_call x0 -> x1, Pallas kernels: none -> 48.2 us  [front(): pl.pallas_call(functools.partial(front_kernel, devices), out_shape=(jax.S...]
    dot_general x4 -> x0, matrix products: 30.2 us -> none  [the longest x1 12.6 us: per_device(): jnp.einsum('chts,cshp->cthp', scores, x_blocks, preferred_element_type=jn...]
    unnamed x20 -> x0, other arithmetic: 29.8 us -> none
    convert_element_type x8 -> x0, other arithmetic: 22.6 us -> none  [the longest x3 8.06 us: conv_silu(): return jax.nn.silu(total).astype(jnp.bfloat16)]
    all_to_all x3 -> x0, starting transfers between devices: 19 us -> none  [the longest x1 7.23 us: per_device(): lax.all_to_all(carry.astype(jnp.bfloat16).reshape(devices, share, P_SIZE,...]
    all_to_all x3 -> x0, waiting for transfers between devices: 12.6 us -> none  [the longest x1 6.94 us: per_device(): lax.all_to_all(jnp.stack(prefix), 'seq', 0, 0)]
    ppermute x2 -> x0, starting transfers between devices: 7.95 us -> none  [shifted(): return lax.ppermute(value, axis, pairs)]
  transfers between devices with their start and end apart: 5 -> 0, of which waited for: 2 -> 0; matrix products, arithmetic and copies ran while one was open for 13% -> 0% of each run, Pallas kernels for 0% -> 0%
where the time goes in v2:
time: 144 us; the launch traced here: 142 us
  Pallas kernels  138 us (96%)
  local copies, waits for them, and re-layouts  3.97 us (3%)
    pallas_call x1, Pallas kernels, project(): pl.pallas_call(functools.partial(project_kernel, rows), out_shape=jax.Sha...  89.4 us
    pallas_call x1, Pallas kernels, front(): pl.pallas_call(functools.partial(front_kernel, devices), out_shape=(jax.S...  48.2 us
    unnamed x2, local copies, waits for them, and re-layouts  3.97 us

profile of v2, /device:TPU:1, one launch (start us, length us, event | category | flops | bytes accessed | tf_op | source)
XLA Modules:
  0.0 141.6 jit_solution(7845337638572303859)
XLA Ops:
  0.0 1.7 %copy.14.dt_ref = bf16[1024,32]{1,0:T(8,128)(2,1)} copy(bf16[1024,32]{0,1:T(8,128)(2,1)} %param.16) | data formatting | bytes 131072 | tf_op args[3]
  1.7 48.2 %front.1 = (f32[1024,2048]{1,0:T(8,128)}, bf16[1024,256]{1,0:T(8,128)(2,1)}, bf16[1024,96]{1,0:T(8,128)(2,1)}, bf16[256,2048]{1,0:T(8,128)(2,1)}) custom-call(bf16[1024,2048]{1,0:T(8,128)(2,1)} %x_ref.1, bf16[2,1024,256]{2,1,0:T(8,128)(2,1)} %bc_ref.1, bf16[1024,32]{1,0:T(8,128)(2,1)} %copy.14.dt_ref, f32[4,2048]{1,0:T(4,128)} %xw_ref.1, ...), custom_call_target="tpu_custom_call" | custom-call | tf_op jit(solution)/shard_map/front/pallas_call | solution.py:260
  49.9 89.4 %project.1 = bf16[128,4096]{1,0:T(8,128)(2,1)} custom-call(f32[1024,2048]{1,0:T(8,128)} %get-tuple-element.9.y_ref, bf16[1024,256]{1,0:T(8,128)(2,1)} %get-tuple-element.10.c_ref, bf16[1024,96]{1,0:T(8,128)(2,1)} %get-tuple-element.11.lead_ref, bf16[256,2048]{1,0:T(8,128)(2,1)} %get-tuple-element.12.incoming_ref, bf16[1024,2048]{1,0:T(8,128)(2,1)} %z_ref.1, ...), custom_call_target="tpu_custom_call" | custom-call | tf_op jit(solution)/shard_map/project/pallas_call | solution.py:464
  139.3 2.3 %copy.16 = bf16[128,4096]{1,0:T(8,128)(2,1)} copy(bf16[128,4096]{1,0:T(8,128)(2,1)} %project.1) | data formatting | bytes 2097152

commit v3 on v2

--- a/solution.py
+++ b/solution.py
@@ -50,16 +50,25 @@
 SCAN_AFTER = 3
 
 
-def front_kernel(devices, x_ref, bc_ref, dt_ref, xw_ref, bw_ref, xb_ref, bb_ref, off_ref, dlog_ref,
+def front_kernel(devices, x_hbm, bc_ref, dtt_ref, xw_ref, bw_ref, xb_ref, bb_ref, off_ref, dlog_ref,
                  skip_ref, y_hbm, c_ref, lead_ref, incoming_ref,
-                 hx, hbc, xf, xc, bt, cumcol, rowt, fend, ec, spread, rowexp, total, carry, before,
+                 x_ref, hx, hbc, xf, xc, bt, cumcol, rowt, fend, ec, spread, rowexp, total, carry, before,
                  stage, ends, got, pref, inc,
-                 hx_sems, hbc_sems, esend, erecv, psend, precv, ysem):
+                 xin, hx_sems, hbc_sems, esend, erecv, psend, precv, ysem):
     me = lax.axis_index("seq")
     tokens, width = x_ref.shape
     blocks = tokens // BLOCK
-    heads = dt_ref.shape[1]
+    heads = dtt_ref.shape[0]
     steps = width // STEP
+
+    def load_x(step):
+        lanes = pl.ds(pl.multiple_of(step * STEP, STEP), STEP)
+        return pltpu.make_async_copy(x_hbm.at[:, lanes], x_ref.at[:, lanes], xin.at[step])
+
+    @pl.loop(0, steps)
+    def _(k):
+        load_x(lax.rem(me // 2 + 1 + k, steps)).start()
+
     barrier = pltpu.get_barrier_semaphore()
 
     @pl.loop(1, devices)
@@ -71,7 +80,7 @@
 
     after = {"seq": lax.rem(me + 1, devices)}
     halo_x = pltpu.make_async_remote_copy(
-        src_ref=x_ref.at[tokens - 16 :, :], dst_ref=hx, send_sem=hx_sems.at[0],
+        src_ref=x_hbm.at[tokens - 16 :, :], dst_ref=hx, send_sem=hx_sems.at[0],
         recv_sem=hx_sems.at[1], device_id=after, device_id_type=MESH)
     halo_bc = pltpu.make_async_remote_copy(
         src_ref=bc_ref.at[:, tokens - 16 :, :], dst_ref=hbc, send_sem=hbc_sems.at[0],
@@ -80,7 +89,7 @@
     halo_x.start()
 
     spread[...] = spreading(heads)
-    steps_dt = dt_ref[...].astype(F32) + off_ref[...]
+    steps_dt = dtt_ref[...].astype(F32).T + off_ref[...]
     steps_dt = jnp.maximum(steps_dt, 0.0) + jnp.log1p(jnp.exp(-jnp.abs(steps_dt)))
     log_decay = steps_dt * (-LOG2E * jnp.exp(dlog_ref[...]))
     at = lax.broadcasted_iota(jnp.int32, (BLOCK, BLOCK), 0)
@@ -149,6 +158,7 @@
         step = lax.rem(me // 2 + 1 + k, steps)
         lane0 = pl.multiple_of(step * STEP, STEP)
         lanes = pl.ds(lane0, STEP)
+        load_x(step).wait()
         xf[0:8, :] = hx[8:16, lanes].astype(F32) * first
         xf[8:, :] = x_ref[:, lanes].astype(F32)
         weights = [xw_ref[i : i + 1, lanes] for i in range(KW)]
@@ -253,7 +263,7 @@
 
 def front(devices, x, bc, dt, xw, bw, xb, bb, offset, decay_log, skip):
     tokens, width = x.shape
-    heads = dt.shape[1]
+    heads = dt.shape[0]
     blocks = tokens // BLOCK
     dma = pltpu.SemaphoreType.DMA
     vmem = pl.BlockSpec(memory_space=pltpu.VMEM)
@@ -265,9 +275,10 @@
             jax.ShapeDtypeStruct((tokens, 3 * heads), BF16),
             jax.ShapeDtypeStruct((N, width), BF16),
         ),
-        in_specs=[vmem] * 10,
+        in_specs=[pl.BlockSpec(memory_space=pl.ANY)] + [vmem] * 9,
         out_specs=(pl.BlockSpec(memory_space=pl.ANY), vmem, vmem, vmem),
         scratch_shapes=[
+            pltpu.VMEM((tokens, width), BF16),
             pltpu.VMEM((16, width), BF16),
             pltpu.VMEM((2, 16, N), BF16),
             pltpu.VMEM((8 + tokens, STEP), F32),
@@ -287,6 +298,7 @@
             pltpu.VMEM((devices, N + 16, 128), BF16),
             pltpu.VMEM((devices, N, 128), BF16),
             pltpu.VMEM((devices, N, 128), BF16),
+            dma((width // STEP,)),
             dma((2,)),
             dma((2,)),
             dma((devices,)),
@@ -302,21 +314,24 @@
     )(x, bc, dt, xw, bw, xb, bb, offset, decay_log, skip)
 
 
-CHUNKS = 4
 TILE = 256
-
-
-def project_kernel(rows, y_ref, c_ref, lead_ref, incoming_ref, z_ref, gain_ref, weight_ref, out_ref,
-                   ybuf, zbuf, spread, gated, normed, w, sent, got, kept, xsent, xgot,
-                   ysem, zsem, wsem, send_sem, recv_sem, xsend_sem, xrecv_sem):
+SIDE = 7 * TILE
+HALF = SIDE // 2
+CHUNK = 3 * TILE
+CHUNKS = 3
+
+
+def project_kernel(rows, y_ref, c_ref, lead_ref, incoming_ref, z_ref, gain_ref, weight_ref, out_hbm,
+                   ybuf, zbuf, spread, gated, normed, wside, w, sent, got, kept, xsent, xgot,
+                   sidesent, sidegot, own, turnsent, turngot, out,
+                   ysem, zsem, wsem, send_sem, recv_sem, xsend_sem, xrecv_sem,
+                   side_send, side_recv, turn_send, turn_recv, osem):
     head = lax.axis_index("head")
     y = head // 2
     x = lax.rem(head, 2)
-    wide = out_ref.shape[1] // CHUNKS
     up = {"head": lax.rem(y + 1, 4) * 2 + x}
     down = {"head": lax.rem(y + 3, 4) * 2 + x}
     across = {"head": y * 2 + 1 - x}
-    blocks = y_ref.shape[0] // rows
     width = y_ref.shape[1]
 
     def needed(s):
@@ -330,19 +345,25 @@
             copies.append(pltpu.make_async_copy(z_ref.at[here, :], zbuf.at[block], zsem.at[block]))
         return copies
 
+    def column(c):
+        return SIDE + c * CHUNK
+
+    def load(c):
+        return pltpu.make_async_copy(
+            weight_ref.at[:, column(c) : column(c) + CHUNK], w.at[c], wsem.at[c])
+
+    side_load = pltpu.make_async_copy(weight_ref.at[:, :SIDE], wside, wsem.at[CHUNKS])
     for copy in rows_in(0):
         copy.start()
-    loads = []
-    for c in range(CHUNKS):
-        load = pltpu.make_async_copy(
-            weight_ref.at[:, c * wide : (c + 1) * wide], w.at[c], wsem.at[c]
-        )
-        load.start()
-        loads.append(load)
-        if c == 0:
-            for s in range(1, 4):
-                for copy in rows_in(s):
-                    copy.start()
+    load(0).start()
+    side_load.start()
+    for copy in rows_in(1):
+        copy.start()
+    for c in range(1, CHUNKS):
+        load(c).start()
+    for s in (2, 3):
+        for copy in rows_in(s):
+            copy.start()
     spread[...] = spreading(lead_ref.shape[1] // 3)
 
     def normalise(block):
@@ -365,6 +386,15 @@
             lanes = slice(t * TILE, (t + 1) * TILE)
             normed[here, lanes] = (gated[:, lanes] * scale * gain_ref[:, lanes]).astype(BF16)
 
+    def normalise_both(s):
+        for copy in rows_in(s):
+            copy.wait()
+        block0, block1 = needed(s)
+
+        @pl.loop(0, 2)
+        def _(role):
+            normalise(jnp.where(role == 0, block0, block1))
+
     barrier = pltpu.get_barrier_semaphore()
     for to in (up, down, across):
         pl.semaphore_signal(barrier, inc=1, device_id=to, device_id_type=MESH)
@@ -390,41 +420,84 @@
             device_id_type=MESH,
         )
 
+    def side_cross(s):
+        return pltpu.make_async_remote_copy(
+            src_ref=sidesent.at[s],
+            dst_ref=sidegot.at[s],
+            send_sem=side_send.at[s],
+            recv_sem=side_recv.at[s],
+            device_id=across,
+            device_id_type=MESH,
+        )
+
+    def turn(r, way):
+        return pltpu.make_async_remote_copy(
+            src_ref=turnsent.at[r, way],
+            dst_ref=turngot.at[r, way],
+            send_sem=turn_send.at[r, way],
+            recv_sem=turn_recv.at[r, way],
+            device_id=up if way == 0 else down,
+            device_id_type=MESH,
+        )
+
+    def pair(s, weight):
+        row0, row1 = (pl.multiple_of(block * rows, rows) for block in needed(s))
+        left = jnp.concatenate(
+            [normed[pl.ds(row0, rows), :], normed[pl.ds(row1, rows), :]], axis=0)
+        part = dot(left, weight)
+        return part[:rows], part[rows:]
+
+    def side_event(s):
+        if s == 0:
+            side_load.wait()
+
+        @pl.loop(0, SIDE // TILE)
+        def _(t):
+            cols = pl.ds(pl.multiple_of(t * TILE, TILE), TILE)
+            part0, part1 = pair(s, wside[:, cols])
+            sidesent[s, :, cols] = part0.astype(BF16)
+            own[s, :, cols] = part1
+
+        side_cross(s).start()
+
+    def turn_event(r):
+        for s in {0: (0, 2), 1: (1,), 2: (), 3: (3,)}[r]:
+            side_cross(s).wait_recv()
+        for way in (0, 1):
+            cols = slice(way * HALF, (way + 1) * HALF)
+            back = (2 - r) % 4
+            mine, theirs = (back, r) if way == 0 else (r, back)
+            value = own[mine, :, cols] + sidegot[theirs, :, cols].astype(F32)
+            if r > 0:
+                turn(r - 1, way).wait_recv()
+                value = value + turngot[r - 1, way].astype(F32)
+            if r < 3:
+                turnsent[r, way] = value.astype(BF16)
+                turn(r, way).start()
+            else:
+                out[:, cols] = value.astype(BF16)
+        if r == 3:
+            store(CHUNKS).start()
+
     def event(c, s):
         if s == 0:
-            loads[c].wait()
-        if c == 0:
-            for copy in rows_in(s):
-                copy.wait()
-
-            @pl.loop(0, 2)
-            def _(role):
-                block0, block1 = needed(s)
-                normalise(jnp.where(role == 0, block0, block1))
-
-        if s > 0:
+            load(c).wait()
+        else:
             for role in (0, 1):
                 ring(c, s - 1, role).wait_recv()
-        block0, block1 = needed(s)
-        row0 = pl.multiple_of(block0 * rows, rows)
-        row1 = pl.multiple_of(block1 * rows, rows)
-
-        @pl.loop(0, wide // TILE)
+
+        @pl.loop(0, CHUNK // TILE)
         def _(t):
             cols = pl.ds(pl.multiple_of(t * TILE, TILE), TILE)
-            left = jnp.concatenate(
-                [normed[pl.ds(row0, rows), :], normed[pl.ds(row1, rows), :]], axis=0
-            )
-            part = jnp.dot(left, w[c, :, cols], preferred_element_type=jnp.float32)
-            part0, part1 = part[:rows], part[rows:]
+            part0, part1 = pair(s, w[c, :, cols])
             if s > 0:
-                part0 = part0 + got[c, s - 1, 0, :, cols].astype(jnp.float32)
-                part1 = part1 + got[c, s - 1, 1, :, cols].astype(jnp.float32)
+                part0 = part0 + got[c, s - 1, 0, :, cols].astype(F32)
+                part1 = part1 + got[c, s - 1, 1, :, cols].astype(F32)
             if s < 3:
-                sent[c, s, 0, :, cols] = part0.astype(jnp.bfloat16)
-                sent[c, s, 1, :, cols] = part1.astype(jnp.bfloat16)
+                sent[c, s, 0, :, cols] = part0.astype(BF16)
+                sent[c, s, 1, :, cols] = part1.astype(BF16)
             else:
-                xsent[c, :, cols] = part0.astype(jnp.bfloat16)
+                xsent[c, :, cols] = part0.astype(BF16)
                 kept[c, :, cols] = part1
 
         if s < 3:
@@ -433,31 +506,51 @@
         else:
             cross(c).start()
 
+    def store(c):
+        cols = slice(0, SIDE) if c == CHUNKS else slice(column(c), column(c) + CHUNK)
+        return pltpu.make_async_copy(out.at[:, cols], out_hbm.at[:, cols], osem.at[c])
+
     def finish(c):
         cross(c).wait_recv()
-        out_ref[:, c * wide : (c + 1) * wide] = (
-            kept[c] + xgot[c].astype(jnp.float32)
-        ).astype(jnp.bfloat16)
-
-    for c, s in ((0, 0), (1, 0), (0, 1), (1, 1), (0, 2), (1, 2), (2, 0), (0, 3), (3, 0), (1, 3),
-                 (2, 1), (3, 1), (2, 2), (3, 2), (2, 3), (3, 3)):
-        event(c, s)
-        if s == 3 and c >= 2:
-            finish(c - 2)
+        out[:, column(c) : column(c) + CHUNK] = (kept[c] + xgot[c].astype(F32)).astype(BF16)
+        store(c).start()
+
+    for s in range(3):
+        normalise_both(s)
+        event(0, s)
+        side_event(s)
+        event(1, s)
+        event(2, s)
+    normalise_both(3)
+    event(0, 3)
+    side_event(3)
+    turn_event(0)
+    event(1, 3)
+    turn_event(1)
+    event(2, 3)
+    turn_event(2)
+    finish(0)
+    finish(1)
+    turn_event(3)
     finish(2)
-    finish(3)
     for c in range(CHUNKS):
         cross(c).wait_send()
         for s in range(3):
             for role in (0, 1):
                 ring(c, s, role).wait_send()
+    for s in range(4):
+        side_cross(s).wait_send()
+    for r in range(3):
+        for way in (0, 1):
+            turn(r, way).wait_send()
+    for c in range(CHUNKS + 1):
+        store(c).wait()
 
 
 def project(y, c_conv, lead, incoming, z, gain, weight):
     tokens, depth = y.shape
     width = weight.shape[1]
     rows = tokens // 8
-    wide = width // CHUNKS
     dma = pltpu.SemaphoreType.DMA
     vmem = pl.BlockSpec(memory_space=pltpu.VMEM)
     far = pl.BlockSpec(memory_space=pl.ANY)
@@ -465,26 +558,38 @@
         functools.partial(project_kernel, rows),
         out_shape=jax.ShapeDtypeStruct((rows, width), BF16),
         in_specs=[far, vmem, vmem, vmem, far, vmem, far],
-        out_specs=vmem,
+        out_specs=far,
         scratch_shapes=[
             pltpu.VMEM((8, rows, depth), F32),
             pltpu.VMEM((8, rows, depth), BF16),
             pltpu.VMEM((lead.shape[1], depth), BF16),
             pltpu.VMEM((rows, depth), F32),
             pltpu.VMEM((tokens, depth), BF16),
-            pltpu.VMEM((CHUNKS, depth, wide), BF16),
-            pltpu.VMEM((CHUNKS, 3, 2, rows, wide), BF16),
-            pltpu.VMEM((CHUNKS, 3, 2, rows, wide), BF16),
-            pltpu.VMEM((CHUNKS, rows, wide), F32),
-            pltpu.VMEM((CHUNKS, rows, wide), BF16),
-            pltpu.VMEM((CHUNKS, rows, wide), BF16),
+            pltpu.VMEM((depth, SIDE), BF16),
+            pltpu.VMEM((CHUNKS, depth, CHUNK), BF16),
+            pltpu.VMEM((CHUNKS, 3, 2, rows, CHUNK), BF16),
+            pltpu.VMEM((CHUNKS, 3, 2, rows, CHUNK), BF16),
+            pltpu.VMEM((CHUNKS, rows, CHUNK), F32),
+            pltpu.VMEM((CHUNKS, rows, CHUNK), BF16),
+            pltpu.VMEM((CHUNKS, rows, CHUNK), BF16),
+            pltpu.VMEM((4, rows, SIDE), BF16),
+            pltpu.VMEM((4, rows, SIDE), BF16),
+            pltpu.VMEM((4, rows, SIDE), F32),
+            pltpu.VMEM((3, 2, rows, HALF), BF16),
+            pltpu.VMEM((3, 2, rows, HALF), BF16),
+            pltpu.VMEM((rows, width), BF16),
             dma((8,)),
             dma((8,)),
-            dma((CHUNKS,)),
+            dma((CHUNKS + 1,)),
             dma((CHUNKS, 3, 2)),
             dma((CHUNKS, 3, 2)),
             dma((CHUNKS,)),
             dma((CHUNKS,)),
+            dma((4,)),
+            dma((4,)),
+            dma((3, 2)),
+            dma((3, 2)),
+            dma((CHUNKS + 1,)),
         ],
         compiler_params=pltpu.CompilerParams(
             collective_id=1, has_side_effects=True, vmem_limit_bytes=63 * 1024 * 1024
@@ -512,7 +617,7 @@
         lax.axis_size("seq"),
         x_values,
         bc_values,
-        dt_values,
+        dt_values.T,
         xconv_weight,
         bconv_weight,
         xconv_bias[None, :],

time: 144 us -> 121 us (0.84)
  Pallas kernels: 138 us -> 117 us
  local copies, waits for them, and re-layouts: 3.97 us -> 2.29 us
    pallas_call x1, Pallas kernels: 89.4 us -> 69 us  [project(): pl.pallas_call(functools.partial(project_kernel, rows), out_shape=jax.Sha...]
    unnamed x2 -> x1, local copies, waits for them, and re-layouts: 3.97 us -> 2.29 us
where the time goes in v3:
time: 121 us; the launch traced here: 119 us
  Pallas kernels  117 us (97%)
  local copies, waits for them, and re-layouts  2.29 us (2%)
    pallas_call x1, Pallas kernels, project(): pl.pallas_call(functools.partial(project_kernel, rows), out_shape=jax.Sha...  69 us
    pallas_call x1, Pallas kernels, front(): pl.pallas_call(functools.partial(front_kernel, devices), out_shape=(jax.S...  47.6 us

profile of v3, /device:TPU:1, one launch (start us, length us, event | category | flops | bytes accessed | tf_op | source)
XLA Modules:
  0.0 118.9 jit_solution(2289006952978706715)
XLA Ops:
  0.0 47.6 %front.1 = (f32[1024,2048]{1,0:T(8,128)}, bf16[1024,256]{1,0:T(8,128)(2,1)}, bf16[1024,96]{1,0:T(8,128)(2,1)}, bf16[256,2048]{1,0:T(8,128)(2,1)}) custom-call(bf16[1024,2048]{1,0:T(8,128)(2,1)} %x_hbm.1, bf16[2,1024,256]{2,1,0:T(8,128)(2,1)} %bc_ref.1, bf16[32,1024]{1,0:T(8,128)(2,1)} %bitcast.6, f32[4,2048]{1,0:T(4,128)} %xw_ref.1, f32[2,4,256]{2,1,0:T(4,128)} %bw_ref.1, ...), custom_call_target="tpu_custom_call" | custom-call | tf_op jit(solution)/shard_map/front/pallas_call | solution.py:270
  47.6 69.0 %project.1 = bf16[128,4096]{1,0:T(8,128)(2,1)} custom-call(f32[1024,2048]{1,0:T(8,128)} %get-tuple-element.9.y_ref, bf16[1024,256]{1,0:T(8,128)(2,1)} %get-tuple-element.10.c_ref, bf16[1024,96]{1,0:T(8,128)(2,1)} %get-tuple-element.11.lead_ref, bf16[256,2048]{1,0:T(8,128)(2,1)} %get-tuple-element.12.incoming_ref, bf16[1024,2048]{1,0:T(8,128)(2,1)} %z_ref.1, ...), custom_call_target="tpu_custom_call" | custom-call | tf_op jit(solution)/shard_map/project/pallas_call | solution.py:557
  116.6 2.3 %copy.15 = bf16[128,4096]{1,0:T(8,128)(2,1)} copy(bf16[128,4096]{1,0:T(8,128)(2,1)} %project.1) | data formatting | bytes 2097152

commit v4 on v3

--- a/solution.py
+++ b/solution.py
@@ -47,19 +47,20 @@
 
 
 STEP = 256
-SCAN_AFTER = 3
+LAG = 3
 
 
 def front_kernel(devices, x_hbm, bc_ref, dtt_ref, xw_ref, bw_ref, xb_ref, bb_ref, off_ref, dlog_ref,
                  skip_ref, y_hbm, c_ref, lead_ref, incoming_ref,
-                 x_ref, hx, hbc, xf, xc, bt, cumcol, rowt, fend, ec, spread, rowexp, total, carry, before,
+                 x_ref, hx, hbc, xf, xc, bt, cumcol, rowt, fend, ec, spread, rowexp, leads, factors, carry, before,
                  stage, ends, got, pref, inc,
-                 xin, hx_sems, hbc_sems, esend, erecv, psend, precv, ysem):
+                 xin, hx_sems, hbc_sems, lead_sems, esend, erecv, psend, precv, ysem):
     me = lax.axis_index("seq")
     tokens, width = x_ref.shape
     blocks = tokens // BLOCK
     heads = dtt_ref.shape[0]
     steps = width // STEP
+    share = N // devices
 
     def load_x(step):
         lanes = pl.ds(pl.multiple_of(step * STEP, STEP), STEP)
@@ -67,7 +68,7 @@
 
     @pl.loop(0, steps)
     def _(k):
-        load_x(lax.rem(me // 2 + 1 + k, steps)).start()
+        load_x(k).start()
 
     barrier = pltpu.get_barrier_semaphore()
 
@@ -110,17 +111,21 @@
         lead_ref[here, :] = split(jnp.exp2(cumul + lead))
         rows_of.append(jnp.exp2(end))
         lead = lead + end
-    rows_of += [jnp.exp2(lead), skip_ref[...]]
+    leads[me] = jnp.broadcast_to(
+        jnp.concatenate([lead, jnp.zeros((1, 128 - heads), F32)], axis=1), (8, 128))
+
+    def send_lead(target):
+        return pltpu.make_async_remote_copy(
+            src_ref=leads.at[me], dst_ref=leads.at[me], send_sem=lead_sems.at[0],
+            recv_sem=lead_sems.at[1], device_id={"seq": target}, device_id_type=MESH)
+
+    @pl.loop(1, devices)
+    def _(k):
+        send_lead(lax.rem(me + k, devices)).start()
+
+    rows_of += [skip_ref[...]]
     rows_of += [jnp.zeros((1, heads), F32)] * (16 - len(rows_of))
     rowexp[...] = dot(split(jnp.concatenate(rows_of, axis=0)), spread[...])
-    whole = rowexp[blocks : blocks + 1, :]
-    high = whole.astype(BF16).astype(F32)
-    middle = (whole - high).astype(BF16).astype(F32)
-    low = whole - high - middle
-    row = lax.broadcasted_iota(jnp.int32, (16, width), 0)
-    total[...] = jnp.where(
-        row == 0, high, jnp.where(row == 1, middle, jnp.where(row == 2, low, 0.0))
-    ).astype(BF16)
 
     first = jnp.where(me > 0, 1.0, 0.0).astype(F32)
 
@@ -141,24 +146,50 @@
             else:
                 c_ref[b * BLOCK : (b + 1) * BLOCK, :] = done
 
-    def send_end(owner):
+    def part(device):
+        return pl.ds(pl.multiple_of(device * share, share), share)
+
+    def send(step, source, target, sends, arrivals, other):
         return pltpu.make_async_remote_copy(
-            src_ref=ends.at[owner], dst_ref=got.at[me], send_sem=esend.at[owner],
-            recv_sem=erecv.at[me], device_id={"seq": owner}, device_id_type=MESH)
-
-    def send_prefix(target):
-        return pltpu.make_async_remote_copy(
-            src_ref=pref.at[target], dst_ref=inc.at[me], send_sem=psend.at[target],
-            recv_sem=precv.at[me], device_id={"seq": target}, device_id_type=MESH)
+            src_ref=source.at[step, part(other), :], dst_ref=target.at[step, part(me), :],
+            send_sem=sends.at[step], recv_sem=arrivals.at[step], device_id={"seq": other},
+            device_id_type=MESH)
+
+    def send_all(step, source, target, sends, arrivals):
+        @pl.loop(1, devices)
+        def _(k):
+            send(step, source, target, sends, arrivals, lax.rem(me + k, devices)).start()
+
+        pltpu.make_async_copy(source.at[step, part(me), :], target.at[step, part(me), :],
+                              arrivals.at[step]).start()
+
+    def arrived(step, target, sends, arrivals):
+        pltpu.make_async_remote_copy(
+            src_ref=target.at[step], dst_ref=target.at[step], send_sem=sends.at[step],
+            recv_sem=arrivals.at[step], device_id={"seq": me}, device_id_type=MESH).wait_recv()
+
+    def left(step, source, sends, arrivals):
+        away = source.at[step, 0 : N - share, :]
+        pltpu.make_async_remote_copy(
+            src_ref=away, dst_ref=away, send_sem=sends.at[step],
+            recv_sem=arrivals.at[step], device_id={"seq": me}, device_id_type=MESH).wait_send()
+
+    def scan(step):
+        arrived(step, got, esend, erecv)
+        lanes = pl.ds(pl.multiple_of(step * STEP, STEP), STEP)
+        run = jnp.zeros((share, STEP), F32)
+        for i in range(devices):
+            rows = slice(i * share, (i + 1) * share)
+            pref[step, rows, :] = run.astype(BF16)
+            run = factors[i : i + 1, lanes] * run + got[step, rows, :].astype(F32)
+        send_all(step, pref, inc, psend, precv)
 
     halo_x.wait_recv()
 
     @pl.loop(0, steps)
     def _(k):
-        step = lax.rem(me // 2 + 1 + k, steps)
-        lane0 = pl.multiple_of(step * STEP, STEP)
-        lanes = pl.ds(lane0, STEP)
-        load_x(step).wait()
+        lanes = pl.ds(pl.multiple_of(k * STEP, STEP), STEP)
+        load_x(k).wait()
         xf[0:8, :] = hx[8:16, lanes].astype(F32) * first
         xf[8:, :] = x_ref[:, lanes].astype(F32)
         weights = [xw_ref[i : i + 1, lanes] for i in range(KW)]
@@ -172,14 +203,21 @@
             run = carry[...]
             before[b, :, lanes] = run.astype(BF16)
             carry[...] = rowexp[b : b + 1, lanes] * run + dot(bt[b], weighted)
-        for half in (0, 1):
-            owner = step * 2 + half
-            ends[owner, 0:N, :] = carry[:, half * 128 : (half + 1) * 128].astype(BF16)
-            ends[owner, N:, :] = total[:, pl.ds(pl.multiple_of(lane0 + half * 128, 128), 128)]
-
-            @pl.when(owner != me)
-            def _():
-                send_end(owner).start()
+        ends[k] = carry[...].astype(BF16)
+        send_all(k, ends, got, esend, erecv)
+
+        @pl.when(k == LAG)
+        def _():
+            others = leads.at[0 : devices - 1]
+            pltpu.make_async_remote_copy(
+                src_ref=others, dst_ref=others, send_sem=lead_sems.at[0], recv_sem=lead_sems.at[1],
+                device_id={"seq": me}, device_id_type=MESH).wait()
+            whole = jnp.concatenate([leads[i, 0:1, :] for i in range(devices)], axis=0)
+            factors[...] = dot(split(jnp.exp2(whole[:, :heads])), spread[...])
+
+        @pl.when(k >= LAG)
+        def _():
+            scan(k - LAG)
 
     def store_y(b):
         return pltpu.make_async_copy(
@@ -207,52 +245,23 @@
                 sides.append(dot(jnp.concatenate(scores, axis=1), both))
             y = jnp.concatenate(sides, axis=1)
             y = y + dot(ec[here, :], spread[:, lanes]) * dot(c_here, before[b, :, lanes])
-            y = y + rowexp[blocks + 1 : blocks + 2, lanes] * xc[here, lanes].astype(F32)
+            y = y + rowexp[blocks : blocks + 1, lanes] * xc[here, lanes].astype(F32)
             stage[b, :, lanes] = y
         store_y(b).start()
 
-    pl.loop(0, SCAN_AFTER)(block_step)
-
-    got[me] = ends[me]
-    carry[:, :128] = jnp.zeros((N, 128), F32)
-
-    @pl.loop(0, devices)
-    def _(i):
-        run = carry[:, :128]
-
-        @pl.when(i != me)
+    @pl.loop(0, blocks)
+    def _(b):
+        @pl.when(b < LAG)
         def _():
-            pref[i] = run.astype(BF16)
-            send_prefix(i).start()
-            pltpu.make_async_remote_copy(
-                src_ref=ends.at[i], dst_ref=got.at[i], send_sem=esend.at[i], recv_sem=erecv.at[i],
-                device_id={"seq": i}, device_id_type=MESH).wait_recv()
-
-        @pl.when(i == me)
-        def _():
-            inc[me] = run.astype(BF16)
-
-        factor = jnp.sum(got[i, N:, :].astype(F32), axis=0, keepdims=True)
-        carry[:, :128] = factor * run + got[i, :N, :].astype(F32)
-
-    pl.loop(SCAN_AFTER, blocks)(block_step)
-
-    @pl.loop(1, devices)
-    def _(k):
-        other = lax.rem(me + k, devices)
-        pltpu.make_async_remote_copy(
-            src_ref=pref.at[other], dst_ref=inc.at[other], send_sem=psend.at[other],
-            recv_sem=precv.at[other], device_id={"seq": other}, device_id_type=MESH).wait_recv()
-
-    for j in range(devices):
-        incoming_ref[:, j * 128 : (j + 1) * 128] = inc[j]
-
-    @pl.loop(1, devices)
-    def _(k):
-        other = lax.rem(me + k, devices)
-        send_end(other).wait_send()
-        send_prefix(other).wait_send()
-
+            scan(steps - LAG + b)
+
+        block_step(b)
+
+    for step in range(steps):
+        arrived(step, inc, psend, precv)
+        incoming_ref[:, step * STEP : (step + 1) * STEP] = inc[step]
+        left(step, ends, esend, erecv)
+        left(step, pref, psend, precv)
     halo_bc.wait_send()
     halo_x.wait_send()
 
@@ -290,21 +299,23 @@
             pltpu.VMEM((tokens, 3 * heads), BF16),
             pltpu.VMEM((3 * heads, width), BF16),
             pltpu.VMEM((16, width), F32),
-            pltpu.VMEM((16, width), BF16),
+            pltpu.VMEM((devices, 8, 128), F32),
+            pltpu.VMEM((devices, width), F32),
             pltpu.VMEM((N, STEP), F32),
             pltpu.VMEM((blocks, N, width), BF16),
             pltpu.VMEM((blocks, BLOCK, width), F32),
-            pltpu.VMEM((devices, N + 16, 128), BF16),
-            pltpu.VMEM((devices, N + 16, 128), BF16),
-            pltpu.VMEM((devices, N, 128), BF16),
-            pltpu.VMEM((devices, N, 128), BF16),
+            pltpu.VMEM((width // STEP, N, STEP), BF16),
+            pltpu.VMEM((width // STEP, N, STEP), BF16),
+            pltpu.VMEM((width // STEP, N, STEP), BF16),
+            pltpu.VMEM((width // STEP, N, STEP), BF16),
             dma((width // STEP,)),
             dma((2,)),
             dma((2,)),
-            dma((devices,)),
-            dma((devices,)),
-            dma((devices,)),
-            dma((devices,)),
+            dma((2,)),
+            dma((width // STEP,)),
+            dma((width // STEP,)),
+            dma((width // STEP,)),
+            dma((width // STEP,)),
             dma((blocks,)),
         ],
         compiler_params=pltpu.CompilerParams(

time: 121 us -> 120 us (level); the launches traced: 119 us -> 120 us
    pallas_call x1, Pallas kernels: 47.6 us -> 49.1 us  [front(): pl.pallas_call(functools.partial(front_kernel, devices), out_shape=(jax.S...]
where the time goes in v4:
time: 120 us
  Pallas kernels  118 us (98%)
  local copies, waits for them, and re-layouts  2.29 us (2%)
    pallas_call x1, Pallas kernels, project(): pl.pallas_call(functools.partial(project_kernel, rows), out_shape=jax.Sha...  68.6 us
    pallas_call x1, Pallas kernels, front(): pl.pallas_call(functools.partial(front_kernel, devices), out_shape=(jax.S...  49.1 us

profile of v4, /device:TPU:1, one launch (start us, length us, event | category | flops | bytes accessed | tf_op | source)
XLA Modules:
  0.0 120.1 jit_solution(12197483850378823669)
XLA Ops:
  0.0 49.1 %front.1 = (f32[1024,2048]{1,0:T(8,128)}, bf16[1024,256]{1,0:T(8,128)(2,1)}, bf16[1024,96]{1,0:T(8,128)(2,1)}, bf16[256,2048]{1,0:T(8,128)(2,1)}) custom-call(bf16[1024,2048]{1,0:T(8,128)(2,1)} %x_hbm.1, bf16[2,1024,256]{2,1,0:T(8,128)(2,1)} %bc_ref.1, bf16[32,1024]{1,0:T(8,128)(2,1)} %bitcast.6, f32[4,2048]{1,0:T(4,128)} %xw_ref.1, f32[2,4,256]{2,1,0:T(4,128)} %bw_ref.1, ...), custom_call_target="tpu_custom_call" | custom-call | tf_op jit(solution)/shard_map/front/pallas_call | solution.py:279
  49.1 68.6 %project.1 = bf16[128,4096]{1,0:T(8,128)(2,1)} custom-call(f32[1024,2048]{1,0:T(8,128)} %get-tuple-element.9.y_ref, bf16[1024,256]{1,0:T(8,128)(2,1)} %get-tuple-element.10.c_ref, bf16[1024,96]{1,0:T(8,128)(2,1)} %get-tuple-element.11.lead_ref, bf16[256,2048]{1,0:T(8,128)(2,1)} %get-tuple-element.12.incoming_ref, bf16[1024,2048]{1,0:T(8,128)(2,1)} %z_ref.1, ...), custom_call_target="tpu_custom_call" | custom-call | tf_op jit(solution)/shard_map/project/pallas_call | solution.py:568
  117.8 2.3 %copy.15 = bf16[128,4096]{1,0:T(8,128)(2,1)} copy(bf16[128,4096]{1,0:T(8,128)(2,1)} %project.1) | data formatting | bytes 2097152

commit v5 on v4

--- a/solution.py
+++ b/solution.py
@@ -90,8 +90,10 @@
     halo_x.start()
 
     spread[...] = spreading(heads)
-    steps_dt = dtt_ref[...].astype(F32).T + off_ref[...]
+    steps_dt = dtt_ref[...].astype(F32) + off_ref[...].T
     steps_dt = jnp.maximum(steps_dt, 0.0) + jnp.log1p(jnp.exp(-jnp.abs(steps_dt)))
+    log_dt = LOG2E * jnp.log(steps_dt)
+    steps_dt = steps_dt.T
     log_decay = steps_dt * (-LOG2E * jnp.exp(dlog_ref[...]))
     at = lax.broadcasted_iota(jnp.int32, (BLOCK, BLOCK), 0)
     to = lax.broadcasted_iota(jnp.int32, (BLOCK, BLOCK), 1)
@@ -105,7 +107,7 @@
         cumul = dot(lower, log_decay[here], precision=lax.Precision.HIGHEST)
         end = cumul[BLOCK - 1 :, :]
         cumcol[here, :] = cumul
-        rowt[b] = (cumul - LOG2E * jnp.log(dt_here)).T
+        rowt[b] = cumul.T - log_dt[:, here]
         fend[here, :] = split(jnp.exp2(end - cumul) * dt_here)
         ec[here, :] = split(jnp.exp2(cumul))
         lead_ref[here, :] = split(jnp.exp2(cumul + lead))
@@ -335,7 +337,7 @@
 def project_kernel(rows, y_ref, c_ref, lead_ref, incoming_ref, z_ref, gain_ref, weight_ref, out_hbm,
                    ybuf, zbuf, spread, gated, normed, wside, w, sent, got, kept, xsent, xgot,
                    sidesent, sidegot, own, turnsent, turngot, out,
-                   ysem, zsem, wsem, send_sem, recv_sem, xsend_sem, xrecv_sem,
+                   ysem, zsem, wsem, side_in, send_sem, recv_sem, xsend_sem, xrecv_sem,
                    side_send, side_recv, turn_send, turn_recv, osem):
     head = lax.axis_index("head")
     y = head // 2
@@ -363,18 +365,13 @@
         return pltpu.make_async_copy(
             weight_ref.at[:, column(c) : column(c) + CHUNK], w.at[c], wsem.at[c])
 
-    side_load = pltpu.make_async_copy(weight_ref.at[:, :SIDE], wside, wsem.at[CHUNKS])
+    def side_load(t):
+        cols = pl.ds(pl.multiple_of(t * TILE, TILE), TILE)
+        return pltpu.make_async_copy(weight_ref.at[:, cols], wside.at[:, cols], side_in.at[t])
+
     for copy in rows_in(0):
         copy.start()
     load(0).start()
-    side_load.start()
-    for copy in rows_in(1):
-        copy.start()
-    for c in range(1, CHUNKS):
-        load(c).start()
-    for s in (2, 3):
-        for copy in rows_in(s):
-            copy.start()
     spread[...] = spreading(lead_ref.shape[1] // 3)
 
     def normalise(block):
@@ -400,6 +397,12 @@
     def normalise_both(s):
         for copy in rows_in(s):
             copy.wait()
+        if s == 0:
+            for t in range(SIDE // TILE):
+                side_load(t).start()
+        elif s < 3:
+            for copy in rows_in(s + 1):
+                copy.start()
         block0, block1 = needed(s)
 
         @pl.loop(0, 2)
@@ -459,11 +462,10 @@
         return part[:rows], part[rows:]
 
     def side_event(s):
-        if s == 0:
-            side_load.wait()
-
         @pl.loop(0, SIDE // TILE)
         def _(t):
+            if s == 0:
+                side_load(t).wait()
             cols = pl.ds(pl.multiple_of(t * TILE, TILE), TILE)
             part0, part1 = pair(s, wside[:, cols])
             sidesent[s, :, cols] = part0.astype(BF16)
@@ -493,6 +495,12 @@
     def event(c, s):
         if s == 0:
             load(c).wait()
+            if c == 0:
+                load(1).start()
+                load(2).start()
+            elif c == 1:
+                for copy in rows_in(1):
+                    copy.start()
         else:
             for role in (0, 1):
                 ring(c, s - 1, role).wait_recv()
@@ -591,7 +599,8 @@
             pltpu.VMEM((rows, width), BF16),
             dma((8,)),
             dma((8,)),
-            dma((CHUNKS + 1,)),
+            dma((CHUNKS,)),
+            dma((SIDE // TILE,)),
             dma((CHUNKS, 3, 2)),
             dma((CHUNKS, 3, 2)),
             dma((CHUNKS,)),

time: 120 us -> 120 us (level)
  no operation moved by 1% of the time
where the time goes in v5:
time: 120 us; the launch traced here: 119 us
  Pallas kernels  117 us (98%)
  local copies, waits for them, and re-layouts  2.29 us (2%)
    pallas_call x1, Pallas kernels, project(): pl.pallas_call(functools.partial(project_kernel, rows), out_shape=jax.Sha...  67.7 us
    pallas_call x1, Pallas kernels, front(): pl.pallas_call(functools.partial(front_kernel, devices), out_shape=(jax.S...  49.3 us

profile of v5, /device:TPU:1, one launch (start us, length us, event | category | flops | bytes accessed | tf_op | source)
XLA Modules:
  0.0 119.3 jit_solution(17474735049194472085)
XLA Ops:
  0.0 49.3 %front.1 = (f32[1024,2048]{1,0:T(8,128)}, bf16[1024,256]{1,0:T(8,128)(2,1)}, bf16[1024,96]{1,0:T(8,128)(2,1)}, bf16[256,2048]{1,0:T(8,128)(2,1)}) custom-call(bf16[1024,2048]{1,0:T(8,128)(2,1)} %x_hbm.1, bf16[2,1024,256]{2,1,0:T(8,128)(2,1)} %bc_ref.1, bf16[32,1024]{1,0:T(8,128)(2,1)} %bitcast.6, f32[4,2048]{1,0:T(4,128)} %xw_ref.1, f32[2,4,256]{2,1,0:T(4,128)} %bw_ref.1, ...), custom_call_target="tpu_custom_call" | custom-call | tf_op jit(solution)/shard_map/front/pallas_call | solution.py:281
  49.3 67.7 %project.1 = bf16[128,4096]{1,0:T(8,128)(2,1)} custom-call(f32[1024,2048]{1,0:T(8,128)} %get-tuple-element.9.y_ref, bf16[1024,256]{1,0:T(8,128)(2,1)} %get-tuple-element.10.c_ref, bf16[1024,96]{1,0:T(8,128)(2,1)} %get-tuple-element.11.lead_ref, bf16[256,2048]{1,0:T(8,128)(2,1)} %get-tuple-element.12.incoming_ref, bf16[1024,2048]{1,0:T(8,128)(2,1)} %z_ref.1, ...), custom_call_target="tpu_custom_call" | custom-call | tf_op jit(solution)/shard_map/project/pallas_call | solution.py:576
  117.0 2.3 %copy.15 = bf16[128,4096]{1,0:T(8,128)(2,1)} copy(bf16[128,4096]{1,0:T(8,128)(2,1)} %project.1) | data formatting | bytes 2097152

commit v6 on v5

--- a/solution.py
+++ b/solution.py
@@ -542,12 +542,12 @@
         event(2, s)
     normalise_both(3)
     event(0, 3)
+    turn_event(0)
     side_event(3)
-    turn_event(0)
+    turn_event(1)
     event(1, 3)
-    turn_event(1)
+    turn_event(2)
     event(2, 3)
-    turn_event(2)
     finish(0)
     finish(1)
     turn_event(3)

time: 120 us -> 120 us (level)
  no operation moved by 1% of the time
where the time goes in v6:
time: 120 us; the launch traced here: 119 us
  Pallas kernels  117 us (98%)
  local copies, waits for them, and re-layouts  2.29 us (2%)
    pallas_call x1, Pallas kernels, project(): pl.pallas_call(functools.partial(project_kernel, rows), out_shape=jax.Sha...  67.6 us
    pallas_call x1, Pallas kernels, front(): pl.pallas_call(functools.partial(front_kernel, devices), out_shape=(jax.S...  49.3 us

profile of v6, /device:TPU:1, one launch (start us, length us, event | category | flops | bytes accessed | tf_op | source)
XLA Modules:
  0.0 119.2 jit_solution(16894388467150747660)
XLA Ops:
  0.0 49.3 %front.1 = (f32[1024,2048]{1,0:T(8,128)}, bf16[1024,256]{1,0:T(8,128)(2,1)}, bf16[1024,96]{1,0:T(8,128)(2,1)}, bf16[256,2048]{1,0:T(8,128)(2,1)}) custom-call(bf16[1024,2048]{1,0:T(8,128)(2,1)} %x_hbm.1, bf16[2,1024,256]{2,1,0:T(8,128)(2,1)} %bc_ref.1, bf16[32,1024]{1,0:T(8,128)(2,1)} %bitcast.6, f32[4,2048]{1,0:T(4,128)} %xw_ref.1, f32[2,4,256]{2,1,0:T(4,128)} %bw_ref.1, ...), custom_call_target="tpu_custom_call" | custom-call | tf_op jit(solution)/shard_map/front/pallas_call | solution.py:281
  49.3 67.6 %project.1 = bf16[128,4096]{1,0:T(8,128)(2,1)} custom-call(f32[1024,2048]{1,0:T(8,128)} %get-tuple-element.9.y_ref, bf16[1024,256]{1,0:T(8,128)(2,1)} %get-tuple-element.10.c_ref, bf16[1024,96]{1,0:T(8,128)(2,1)} %get-tuple-element.11.lead_ref, bf16[256,2048]{1,0:T(8,128)(2,1)} %get-tuple-element.12.incoming_ref, bf16[1024,2048]{1,0:T(8,128)(2,1)} %z_ref.1, ...), custom_call_target="tpu_custom_call" | custom-call | tf_op jit(solution)/shard_map/project/pallas_call | solution.py:576
  116.9 2.3 %copy.15 = bf16[128,4096]{1,0:T(8,128)(2,1)} copy(bf16[128,4096]{1,0:T(8,128)(2,1)} %project.1) | data formatting | bytes 2097152
